TPU v7x, 512 devices: a whole 4x4x16 slice. The times are simulated.
512 devices in a mesh: ctx: 64 (over z, y), head: 8 (over x, core).
Axes of the slice: x: 4, y: 4, z: 16, core: 2. Of those that a mesh axis runs over, the one named last changes fastest.
Arguments:
- queries: bfloat16 [32768, 2048], P('ctx', 'head'), may hold values from -12 to 12
- keys: bfloat16 [32768, 2048], P('ctx', 'head'), may hold values from -12 to 12
- values: bfloat16 [32768, 4096], P('ctx', 'head'), may hold values from -6 to 6
- input_pre: float32 [32768, 8], P('ctx', 'head'), may hold values from -6 to 98
- forget_pre: float32 [32768, 8], P('ctx', 'head'), may hold values from -2 to 16
- output_pre: float32 [32768, 8], P('ctx', 'head'), may hold values from -8 to 8
- w_out: bfloat16 [4096, 4096], P('ctx', 'head'), may hold values from -0.25 to 0.25
Outputs:
- layer_out: bfloat16 [32768, 4096], P('ctx', 'head')
All inputs are finite; a program needn't handle non-finite values.
Results may differ from a plain program's by a relative error of at most 0.0062.
Values may be sent and summed in bfloat16 or wider, within the bound.
A program may use at most 128 MiB of HBM per device.

v0:
```python
import jax
import jax.numpy as jnp
from jax import lax
from jax.sharding import PartitionSpec as P


def carried_in(part, axis, combine, identity):
    place = lax.axis_index(axis)
    gathered = jax.tree.map(lambda a: lax.all_gather(a, axis), part)
    state = jax.tree.map(lambda a, e: jnp.zeros_like(a) + jnp.asarray(e, a.dtype), part, identity)

    def one(hop, state):
        return combine(
            state, jax.tree.map(lambda a: lax.dynamic_index_in_dim(a, hop, 0, False), gathered)
        )

    return lax.fori_loop(0, place, one, state)


def combine(earlier, later):
    mem_a, norm_a, top_a, decay_a = earlier
    mem_b, norm_b, top_b, decay_b = later
    top_log = jnp.maximum(decay_b + top_a, top_b)
    keep_old = jnp.exp(decay_b + top_a - top_log)
    fresh_w = jnp.exp(top_b - top_log)
    return (
        keep_old * mem_a + fresh_w * mem_b,
        keep_old * norm_a + fresh_w * norm_b,
        top_log,
        decay_a + decay_b,
    )


def local(queries, keys, values, input_pre, forget_pre, output_pre, w_out):
    tok_rows, width_k = queries.shape
    width_v = values.shape[1]
    score_scale = width_k ** (-0.5)
    input_gain = input_pre[:, 0]
    log_forget_gate = jax.nn.log_sigmoid(forget_pre[:, 0])
    cum_decay = jnp.cumsum(log_forget_gate)
    block_decay = cum_decay[-1:]
    rest_gain = block_decay - cum_decay + input_gain
    top_local = jnp.max(rest_gain, keepdims=True)
    key_weight = jnp.exp(rest_gain - top_local)
    scaled = keys.astype(jnp.float32) * key_weight[:, None]
    memory_local = lax.dot_general(
        scaled.astype(jnp.bfloat16),
        values,
        (((0,), (0,)), ((), ())),
        preferred_element_type=jnp.float32,
    )
    norm_local = jnp.sum(scaled, axis=0)
    identity = (
        jnp.zeros((width_k, width_v), jnp.float32),
        jnp.zeros((width_k,), jnp.float32),
        jnp.full((1,), -1e30, jnp.float32),
        jnp.zeros((1,), jnp.float32),
    )
    memory, norm_vec, top_prev, _ = carried_in(
        (memory_local, norm_local, top_local, block_decay), "ctx", combine, identity
    )
    scores = (
        lax.dot_general(queries, keys, (((1,), (1,)), ((), ())), preferred_element_type=jnp.float32)
        * score_scale
    )
    causal = jnp.arange(tok_rows)[:, None] >= jnp.arange(tok_rows)[None, :]
    rel_gain = jnp.where(
        causal, cum_decay[:, None] - cum_decay[None, :] + input_gain[None, :], -1e30
    )
    top_tok = jnp.maximum(cum_decay + top_prev, jnp.max(rel_gain, axis=1))
    weighted = jnp.exp(rel_gain - top_tok[:, None]) * scores
    den_in = jnp.sum(weighted, axis=1)
    numerator_input = jnp.dot(
        weighted.astype(jnp.bfloat16), values, preferred_element_type=jnp.float32
    )
    lift = jnp.exp(cum_decay + top_prev - top_tok)
    num_out = (
        jnp.dot(queries, memory.astype(jnp.bfloat16), preferred_element_type=jnp.float32)
        * score_scale
    )
    normalizer_output = (
        jnp.dot(queries.astype(jnp.float32), norm_vec, precision=lax.Precision.HIGHEST)
        * score_scale
    )
    numer = numerator_input + lift[:, None] * num_out
    denom = jnp.maximum(jnp.abs(den_in + lift * normalizer_output), jnp.exp(-top_tok))
    hidden = numer / denom[:, None]
    gated_out = (jax.nn.sigmoid(output_pre[:, 0])[:, None] * hidden).astype(jnp.bfloat16)
    gated_whole = lax.all_gather(gated_out, "head", axis=1, tiled=True)
    mixed_out = jnp.dot(
        gated_whole,
        lax.all_gather(w_out, "ctx", axis=0, tiled=True),
        preferred_element_type=jnp.float32,
    )
    return mixed_out.astype(jnp.bfloat16)


def solution(mesh):
    in_specs = (
        P("ctx", "head"),
        P("ctx", "head"),
        P("ctx", "head"),
        P("ctx", "head"),
        P("ctx", "head"),
        P("ctx", "head"),
        P("ctx", "head"),
    )
    out_specs = P("ctx", "head")
    return jax.shard_map(local, mesh=mesh, in_specs=in_specs, out_specs=out_specs, check_vma=False)
```

profile of v0, /device:TPU:1, one launch (start us, length us, event | category | flops | bytes accessed | tf_op | source)
XLA Modules:
  0.0 607.0 jit_solution(17969517601513673308)
XLA Ops:
  6.5 0.7 neg.27
  7.3 0.3 reduce-window.9
  7.9 1.3 dynamic-slice
  9.2 1.2 fusion.15
  10.3 0.7 add_subtract_fusion
  11.0 2.0 add_reduce_fusion
  13.0 1.3 subtract_exponential_fusion.1
  14.3 2.2 fusion.9
  16.6 0.7 all-gather.10.cloned.1.call-update
  17.3 1.1 fusion.7
  18.4 77.8 %all-gather.3 = f32[64,1,256]{2,1,0:T(1,128)S(1)} all-gather(f32[1,1,256]{2,1,0:T(1,128)S(1)} %bitcast.65), channel_id=4, replica_groups=mesh['ctx'=64,'head'=8] {'ctx'}, dimensions={0}, use_global_device_ids=true | all-gather | bytes 66560 | tf_op jit(solution)/shard_map/all_gather | solution.py:9
  96.2 1.3 dynamic-update-slice.1
  97.5 118.5 %all-reduce.2 = (f32[64]{0:T(128)S(1)}, f32[64]{0:T(128)S(1)}) all-reduce(f32[64]{0:T(128)S(1)} %get-tuple-element.107, f32[64]{0:T(128)S(1)} %dynamic-update-slice.1), channel_id=2, replica_groups=mesh['ctx'=64,'head'=8] {'ctx'}, use_global_device_ids=true, to_apply=%add | all-reduce | flops 128 | bytes 1024
  216.0 0.9 fusion.5
  216.9 0.7 add_divide_fusion
  217.6 99.3 %all-gather.12.cloned.1.call-done = f32[16384,512]{1,0:T(8,128)} async-done(((f32[256,512]{1,0:T(8,128)}), f32[16384,512]{1,0:T(8,128)}) %all-gather.12.cloned.1.call-update) | async-done | bytes 33554448 | tf_op jit(solution)/shard_map/all_gather | solution.py:9
  317.1 0.9 copy-done.2
  318.0 0.3 fusion.17
  318.3 0.4 fusion.16
  318.7 0.3 fusion.2
  319.0 1.3 fusion.4
  320.4 133.5 %all-gather.10.cloned.1.call-done = bf16[4096,512]{1,0:T(8,128)(2,1)} async-done(((bf16[64,512]{1,0:T(8,128)(2,1)}), bf16[4096,512]{1,0:T(8,128)(2,1)}) %all-gather.10.cloned.1.call-update) | async-done | bytes 4194320 | tf_op jit(solution)/shard_map/all_gather | solution.py:92
  453.9 140.0 %all-gather.8.cloned.1.call-done = bf16[512,4096]{1,0:T(8,128)(2,1)} async-done(((bf16[512,512]{1,0:T(8,128)(2,1)}), bf16[512,4096]{1,0:T(8,128)(2,1)}) %all-gather.8.cloned.1.call-update) | async-done | bytes 4194320 | tf_op jit(solution)/shard_map/all_gather | solution.py:89
  593.9 6.6 %convolution_convert_fusion = bf16[512,512]{1,0:T(8,128)(2,1)} fusion(bf16[512,4096]{1,0:T(8,128)(2,1)} %all-gather.8.cloned.1.call-done, bf16[4096,512]{1,0:T(8,128)(2,1)} %all-gather.10.cloned.1.call-done), kind=kOutput, calls=%fused_computation.12 | convolution fusion | flops 2147745792 | bytes 8912896 | tf_op jit(solution)/shard_map/dot_general | solution.py:90
  (25 shorter events, 0.5 us)
Async XLA Ops:
  6.5 7.8 %copy-start = (bf16[512,512]{1,0:T(8,128)(2,1)S(1)}, bf16[512,512]{1,0:T(8,128)(2,1)}, u32[]{:S(2)}) copy-start(bf16[512,512]{1,0:T(8,128)(2,1)} %param.11) | copy-start | bytes 1572868
  6.5 310.4 %all-gather.12.cloned.1.call-start = ((), (), s32[]{:S(2)}) async-start(), calls=%async_computation.2 | async-start | bytes 34078720 | tf_op jit(solution)/shard_map/all_gather | solution.py:9
  16.5 437.3 %all-gather.10.cloned.1.call-start = ((), (), s32[]{:S(2)}) async-start(), calls=%async_computation.1 | async-start | bytes 4259840 | tf_op jit(solution)/shard_map/all_gather | solution.py:92
  17.3 576.6 %all-gather.8.cloned.1.call-start = ((), (), s32[]{:S(2)}) async-start(), calls=%async_computation | async-start | bytes 4718592 | tf_op jit(solution)/shard_map/all_gather | solution.py:89
  317.0 1.0 copy-start.2
  317.0 1.2 copy-start.1
  317.1 1.2 copy-start.3
Sparse Core Ops, SparseCore 0:
  16.7 300.2 all-gather.11
  319.9 133.9 all-gather.9
  456.0 137.8 all-gather.7
where the time goes:
time: 612 us; the launch traced here: 607 us
  waiting for transfers between devices  374 us (61%)
  blocking collectives  196 us (32%)
  between operations  13.2 us (2%)
  matrix products  11.1 us (2%)
  other arithmetic  7.88 us (1%)
    all_gather x1, waiting for transfers between devices, local(): gated_whole = lax.all_gather(gated_out, 'head', axis=1, tiled=True)  140 us
    all_gather x1, waiting for transfers between devices, local(): lax.all_gather(w_out, 'ctx', axis=0, tiled=True)  134 us
    unnamed x1, blocking collectives  118 us
    all_gather x1, waiting for transfers between devices, carried_in(): gathered = jax.tree.map(lambda a: lax.all_gather(a, axis), part)  99.3 us
    all_gather x1, blocking collectives, carried_in(): gathered = jax.tree.map(lambda a: lax.all_gather(a, axis), part)  77.8 us
  transfers between devices with their start and end apart: 3, of which 3 were waited for; matrix products, arithmetic and copies ran while one was open for 1% of the time, Pallas kernels for 0%

commit v1 on v0

v1 whole, which is shorter than its diff:
```python
import functools

import jax
import jax.numpy as jnp
from jax import lax
from jax.experimental import pallas as pl
from jax.experimental.pallas import tpu as pltpu
from jax.sharding import PartitionSpec as P

MESH = pl.DeviceIdType.MESH
F32 = jnp.float32
BF16 = jnp.bfloat16
NY = 4
CHUNKS = 4


def _log_sigmoid(f):
    e = jnp.exp(-jnp.abs(f))
    s = e / (2.0 + e)
    s2 = s * s
    poly = jnp.full_like(s, 1.0 / 15.0)
    for d in (13.0, 11.0, 9.0, 7.0, 5.0, 3.0, 1.0):
        poly = poly * s2 + 1.0 / d
    return jnp.minimum(f, 0.0) - 2.0 * s * poly


def _combine_top(top, decay, fresh):
    new = jnp.maximum(decay + top, fresh)
    return new, jnp.exp(decay + top - new), jnp.exp(fresh - new)


def _wide(row, n):
    return jnp.concatenate([row] * n, axis=1)


def kernel(nz, ny, nx, q_ref, k_ref, v_ref, i_ref, f_ref, o_ref, w_ref, out_ref, *scr):
    (mloc, ybuf, sy, tt, stt, ta, sta, pb, sp, pz, mo, sm, mem, gbuf, wbuf, base, gbc, cols,
     s1s, s1r, s1bs, s1br, s3s, s3r, s3bs, s3br, s5s, s5r, s6s, s6r,
     wfs, wfr, wbs, wbr, yps, ypr, yms, ymr, y2s, y2r, xs, xr, bs, br) = scr
    tok, dk = q_ref.shape
    dv = v_ref.shape[1]
    wr = w_ref.shape[0]
    nh = 2 * nx
    qr = dk // ny
    lt = dv // 128
    nt = (qr // 16) * lt
    tpo = nt // nz
    scale = dk ** (-0.5)
    c = lax.axis_index("ctx")
    h = lax.axis_index("head")
    z, y = lax.div(c, ny), lax.rem(c, ny)
    x, core = lax.div(h, 2), lax.rem(h, 2)
    sib = h + 1 - 2 * core

    def zat(d):
        return lax.rem(z + (d + nz), nz)

    def yat(d):
        return lax.rem(y + (d + ny), ny)

    def hat(d):
        return lax.rem(x + (d + nx), nx) * 2 + core

    def dev(zz, yy, hh):
        return (zz * ny + yy, hh)

    def rcopy(src, dst, ss, rs, to):
        return pltpu.make_async_remote_copy(
            src_ref=src, dst_ref=dst, send_sem=ss, recv_sem=rs, device_id=to, device_id_type=MESH
        )

    partners = [dev(z, yat(d), h) for d in range(1, ny)]
    partners += [dev(zat(d), y, h) for d in range(1, nz)]
    if nx > 1:
        partners += [(c, hat(1)), (c, hat(-1))]
    partners += [(c, sib)]
    barrier = pltpu.get_barrier_semaphore()
    for p in partners:
        pl.semaphore_signal(barrier, inc=1, device_id=p, device_id_type=MESH)

    def wpiece(dz, dy):
        row = pl.multiple_of((zat(dz) * ny + yat(dy)) * wr, wr)
        return wbuf.at[pl.ds(row, wr), :]

    nf = nz // 2
    nb = nz - 1 - nf

    def wz(step, sign):
        src = w_ref if step == 1 else wpiece(-sign * (step - 1), 0)
        dst = wpiece(-sign * (step - 1), 0)
        ss, rs = (wfs, wfr) if sign > 0 else (wbs, wbr)
        return rcopy(src, dst, ss.at[step - 1], rs.at[step - 1], dev(zat(sign), y, h))

    def wz_got(step, sign):
        ss, rs = (wfs, wfr) if sign > 0 else (wbs, wbr)
        piece = wpiece(-sign * step, 0)
        return rcopy(piece, piece, ss.at[step - 1], rs.at[step - 1], dev(zat(sign), y, h))

    def wy(j, sign):
        src = w_ref if j == 0 else wpiece(j, 0)
        ss, rs = (yps, ypr) if sign > 0 else (yms, ymr)
        return rcopy(src, wpiece(j, 0), ss.at[j + nf], rs.at[j + nf], dev(z, yat(sign), h))

    def wy_got(j, sign):
        piece = wpiece(j, -sign)
        ss, rs = (yps, ypr) if sign > 0 else (yms, ymr)
        return rcopy(piece, piece, ss.at[j + nf], rs.at[j + nf], dev(z, yat(sign), h))

    def wy2(j):
        sign = 1 if j % 2 == 0 else -1
        piece = wpiece(j, -sign)
        return rcopy(piece, piece, y2s.at[j + nf], y2r.at[j + nf], dev(z, yat(sign), h))

    def wy2_got(j):
        sign = 1 if j % 2 == 0 else -1
        piece = wpiece(j, -2 * sign)
        return rcopy(piece, piece, y2s.at[j + nf], y2r.at[j + nf], dev(z, yat(sign), h))

    rels = list(range(-nf, nb + 1))

    def w_step(step):
        for sign, last in ((1, nf), (-1, nb)):
            if step <= last:
                wz_got(step, sign).wait_recv()
                if step + 1 <= last:
                    wz(step + 1, sign).start()

    def w_across(js):
        if ny > 1:
            for j in js:
                wy(j, 1).start()
                wy(j, -1).start()

    def w_relay(js):
        if ny > 1:
            for j in js:
                for sign in (1, -1):
                    wy_got(j, sign).wait_recv()
                wy2(j).start()

    lane = lax.broadcasted_iota(jnp.int32, (8, tok), 1)
    gate_in = jnp.broadcast_to(i_ref[...], (8, tok))
    cum = _log_sigmoid(jnp.broadcast_to(f_ref[...], (8, tok)))
    sh = 1
    while sh < tok:
        cum = cum + jnp.where(lane >= sh, pltpu.roll(cum, sh, 1), 0.0)
        sh *= 2
    a_row = gate_in - cum
    top_row = a_row
    sh = 1
    while sh < tok:
        top_row = jnp.maximum(top_row, jnp.where(lane >= sh, pltpu.roll(top_row, sh, 1), -3e38))
        sh *= 2
    sig = 1.0 / (1.0 + jnp.exp(-jnp.broadcast_to(o_ref[...], (8, tok))))
    decay = cum[0:1, tok - 1:tok]
    a_last = top_row[0:1, tok - 1:tok]
    kw_row = jnp.exp(a_row - a_last)
    rows = lax.broadcasted_iota(jnp.int32, (128, tok), 0)
    stack = jnp.where(rows == 0, top_row[0:1], jnp.where(rows == 1, cum[0:1],
            jnp.where(rows == 2, sig[0:1], kw_row[0:1])))
    cols[...] = jnp.transpose(stack)
    a1 = a_row[0:1]

    scaled = k_ref[...].astype(F32) * cols[:, 3:4]
    norm = jnp.sum(scaled, axis=0, keepdims=True)
    m_local = lax.dot_general(
        scaled.astype(BF16), v_ref[...], (((0,), (0,)), ((), ())), preferred_element_type=F32
    )
    for j in range(ny):
        mloc[j] = m_local[j * qr:(j + 1) * qr].astype(BF16)
    pad = [jnp.zeros((4, 128), F32)]
    stat = jnp.concatenate(
        [norm[:, 0:128], norm[:, 128:256], jnp.broadcast_to(decay, (1, 128)),
         jnp.broadcast_to(decay + a_last, (1, 128))] + pad, axis=0)
    sy[y] = stat
    ybuf[y] = mloc[y]
    own_rows = pl.multiple_of(c * wr, wr)
    wbuf[pl.ds(own_rows, wr), :] = w_ref[...]

    pl.semaphore_wait(barrier, len(partners))

    def s1(d):
        return rcopy(mloc.at[yat(d)], ybuf.at[y], s1s.at[d - 1], s1r.at[d - 1], dev(z, yat(d), h))

    def s1b(d):
        return rcopy(sy.at[y], sy.at[y], s1bs.at[d - 1], s1br.at[d - 1], dev(z, yat(d), h))

    def s1_got(d):
        return rcopy(mloc.at[y], ybuf.at[yat(-d)], s1s.at[d - 1], s1r.at[d - 1], dev(z, yat(d), h))

    def s1b_got(d):
        return rcopy(sy.at[y], sy.at[yat(-d)], s1bs.at[d - 1], s1br.at[d - 1], dev(z, yat(d), h))

    for d in range(1, ny):
        s1b(d).start()
        s1(d).start()
    if nf:
        wz(1, 1).start()
    if nb:
        wz(1, -1).start()

    rb = 128
    dens = []
    for r in range(tok // rb):
        width = (r + 1) * rb
        sl = pl.ds(r * rb, rb)
        scores = lax.dot_general(
            q_ref[sl, :], k_ref[0:width, :], (((1,), (1,)), ((), ())), preferred_element_type=F32
        ) * scale
        ti = lax.broadcasted_iota(jnp.int32, (rb, width), 0) + r * rb
        si = lax.broadcasted_iota(jnp.int32, (rb, width), 1)
        rel = jnp.where(ti >= si, a1[:, 0:width] - cols[sl, 0:1], -1e30)
        weighted = jnp.exp(rel) * scores
        dens.append(jnp.sum(weighted, axis=1, keepdims=True))
        base[sl, :] = jnp.dot(weighted.astype(BF16), v_ref[0:width, :], preferred_element_type=F32)
    den_loc = jnp.concatenate(dens, axis=0)

    w_step(1)

    for d in range(1, ny):
        s1b_got(d).wait_recv()
        s1_got(d).wait_recv()
    dec = [sy[j, 2:3, :] for j in range(ny)]
    tops = [sy[j, 3:4, :] for j in range(ny)]
    suffix = jnp.zeros((1, 128), F32)
    logs = [None] * ny
    for j in reversed(range(ny)):
        logs[j] = suffix + tops[j]
        suffix = suffix + dec[j]
    top_t = functools.reduce(jnp.maximum, logs)
    wts = [jnp.exp(lg - top_t) for lg in logs]
    total = sum(_wide(wts[j], lt) * ybuf[j].astype(F32) for j in range(ny))
    for t in range(nt):
        a, b = divmod(t, lt)
        o, s = divmod(t, tpo)
        tt[o, s * 16:(s + 1) * 16, :] = total[a * 16:(a + 1) * 16, b * 128:(b + 1) * 128].astype(BF16)
    norm_t = sum(wts[j] * sy[j, 0:2, :] for j in range(ny))
    stt[...] = jnp.concatenate([norm_t, suffix, top_t] + pad, axis=0)
    ta[z] = tt[z]
    sta[z] = stt[...]

    def s3(d):
        return rcopy(tt.at[zat(d)], ta.at[z], s3s.at[d - 1], s3r.at[d - 1], dev(zat(d), y, h))

    def s3b(d):
        return rcopy(stt, sta.at[z], s3bs.at[d - 1], s3br.at[d - 1], dev(zat(d), y, h))

    def s3_got(d):
        return rcopy(tt.at[z], ta.at[zat(-d)], s3s.at[d - 1], s3r.at[d - 1], dev(zat(d), y, h))

    def s3b_got(d):
        return rcopy(stt, sta.at[zat(-d)], s3bs.at[d - 1], s3br.at[d - 1], dev(zat(d), y, h))

    far = sorted(range(1, nz), key=lambda d: -min(d, nz - d))
    for d in far:
        s3b(d).start()
        s3(d).start()

    w_across([0])
    w_step(2)
    w_across([j for j in (-1, 1) if j in rels])
    w_step(3)
    w_across([j for j in (-2, 2) if j in rels])
    w_step(4)

    for d in far:
        s3b_got(d).wait_recv()
        s3_got(d).wait_recv()
    state = jnp.zeros((tpo * 16, 128), F32)
    norm_p = jnp.zeros((2, 128), F32)
    top_p = jnp.full((1, 128), -1e30, F32)
    for zz in range(nz):
        pb[zz] = state.astype(BF16)
        sp[zz, 0:2, :] = norm_p
        sp[zz, 2:3, :] = top_p
        if zz + 1 < nz:
            top_p, keep, fresh = _combine_top(top_p, sta[zz, 2:3, :], sta[zz, 3:4, :])
            state = keep * state + fresh * ta[zz].astype(F32)
            norm_p = keep * norm_p + fresh * sta[zz, 0:2, :]
    pz[z] = pb[z]

    def s5(d):
        return rcopy(pb.at[zat(d)], pz.at[z], s5s.at[d - 1], s5r.at[d - 1], dev(zat(d), y, h))

    def s5_got(d):
        return rcopy(pb.at[z], pz.at[zat(-d)], s5s.at[d - 1], s5r.at[d - 1], dev(zat(d), y, h))

    for d in far:
        s5(d).start()

    norm_p = sp[z, 0:2, :]
    top_p = sp[z, 2:3, :]
    keeps, freshs = [], []
    for j in range(ny):
        sm[j, 0:2, :] = norm_p
        sm[j, 2:3, :] = top_p
        if j + 1 < ny:
            top_p, keep, fresh = _combine_top(top_p, dec[j], tops[j])
            keeps.append(keep)
            freshs.append(fresh)
            norm_p = keep * norm_p + fresh * sy[j, 0:2, :]
    norm_prev = sm[y, 0:2, :]
    top_prev = sm[y, 2:3, :][:, 0:1]
    norm_row = jnp.concatenate([norm_prev[0:1], norm_prev[1:2]], axis=1)
    q_norm = jnp.sum(q_ref[...].astype(F32) * norm_row, axis=1, keepdims=True) * scale
    top_loc = cols[:, 0:1]
    top_mix = jnp.maximum(top_loc, top_prev)
    inner = jnp.exp(top_loc - top_mix)
    lift = jnp.exp(top_prev - top_mix)
    den = jnp.maximum(
        jnp.abs(inner * den_loc + lift * q_norm), jnp.exp(-(cols[:, 1:2] + top_mix)))
    gate = cols[:, 2:3] / den
    base[...] = base[...] * (gate * inner)
    gbc[...] = jnp.broadcast_to(gate * lift * scale, gbc.shape)

    w_across([j for j in (-3, 3) if j in rels])
    w_step(5)
    w_relay([0])
    w_step(6)

    for d in far:
        s5_got(d).wait_recv()
    tiles = [pz[t // tpo, (t % tpo) * 16:(t % tpo + 1) * 16, :].astype(F32) for t in range(nt)]
    state = jnp.concatenate(
        [jnp.concatenate(tiles[a * lt:(a + 1) * lt], axis=1) for a in range(qr // 16)], axis=0)
    for j in range(ny):
        mo[j] = state.astype(BF16)
        if j + 1 < ny:
            state = _wide(keeps[j], lt) * state + _wide(freshs[j], lt) * ybuf[j].astype(F32)
    mem[pl.ds(pl.multiple_of(y * qr, qr), qr), :] = mo[y]

    def s6(d):
        return rcopy(mo.at[yat(d)], mem.at[pl.ds(pl.multiple_of(y * qr, qr), qr), :],
                     s6s.at[d - 1], s6r.at[d - 1], dev(z, yat(d), h))

    def s6_got(d):
        return rcopy(mo.at[y], mem.at[pl.ds(pl.multiple_of(yat(-d) * qr, qr), qr), :],
                     s6s.at[d - 1], s6r.at[d - 1], dev(z, yat(d), h))

    for d in range(1, ny):
        s6(d).start()
    w_step(7)
    w_across([j for j in (-4, -5, 4, 5) if j in rels])
    w_relay([j for j in (-1, 1, -2, 2) if j in rels])
    for d in range(1, ny):
        s6_got(d).wait_recv()

    cr = tok // CHUNKS

    def gchunk(hh, r):
        return gbuf.at[hh, pl.ds(r * cr, cr), :]

    def xcopy(slot, hh, r, to):
        piece = gchunk(hh, r)
        return rcopy(piece, piece, xs.at[slot, r], xr.at[slot, r], to)

    def scopy(slot, hh, r):
        piece = gchunk(hh, r)
        return rcopy(piece, piece, bs.at[slot, r], br.at[slot, r], (c, sib))

    for r in range(CHUNKS):
        sl = pl.ds(r * cr, cr)
        out = jnp.dot(q_ref[sl, :], mem[...], preferred_element_type=F32)
        gbuf[h, sl, :] = (base[sl, :] + _wide(gbc[sl, :], lt) * out).astype(BF16)
        if nx > 1:
            xcopy(0, h, r, (c, hat(1))).start()
            xcopy(1, h, r, (c, hat(-1))).start()
        scopy(0, h, r).start()

    half = CHUNKS // 2
    rest = [j for j in (-6, 6, -7, 7, -8) if j in rels]
    w_step(8)
    w_across(rest)
    if nx > 1:
        for r in range(CHUNKS):
            xcopy(0, hat(-1), r, (c, hat(1))).wait_recv()
            if r < half:
                xcopy(2, hat(-1), r, (c, hat(1))).start()
            scopy(1, hat(-1), r).start()
            xcopy(1, hat(1), r, (c, hat(-1))).wait_recv()
            if r >= half:
                xcopy(2, hat(1), r, (c, hat(-1))).start()
            scopy(2, hat(1), r).start()
            w_relay([j for j in ((-3, 3), (-4, 4), (-5, 5), (-6, 6))[r] if j in rels])
        for r in range(CHUNKS):
            xcopy(2, hat(2), r, (c, hat(1))).wait_recv()
            scopy(3, hat(2), r).start()
    else:
        w_relay([j for j in (-3, 3, -4, 4, -5, 5, -6, 6) if j in rels])
    w_relay([j for j in (-7, 7, -8) if j in rels])
    if ny > 1:
        for j in rels:
            wy2_got(j).wait_recv()
    sib_x = lax.div(sib, 2) * 2 + 1 - core

    def hat_sib(d):
        return lax.rem(x + (d + nx), nx) * 2 + 1 - core

    for r in range(CHUNKS):
        scopy(0, sib_x, r).wait_recv()
        if nx > 1:
            scopy(1, hat_sib(-1), r).wait_recv()
            scopy(2, hat_sib(1), r).wait_recv()
            scopy(3, hat_sib(2), r).wait_recv()

    for rr in range(tok // 256):
        for cc in range(dv // 256):
            acc = jnp.zeros((256, 256), F32)
            for hh in range(nh):
                acc = acc + jnp.dot(
                    gbuf[hh, rr * 256:(rr + 1) * 256, :],
                    wbuf[hh * dv:(hh + 1) * dv, cc * 256:(cc + 1) * 256],
                    preferred_element_type=F32)
            out_ref[rr * 256:(rr + 1) * 256, cc * 256:(cc + 1) * 256] = acc.astype(BF16)

    for d in range(1, ny):
        s1(d).wait_send()
        s1b(d).wait_send()
        s6(d).wait_send()
    for d in range(1, nz):
        s3(d).wait_send()
        s3b(d).wait_send()
        s5(d).wait_send()
    for sign, last in ((1, nf), (-1, nb)):
        for step in range(1, last + 1):
            wz(step, sign).wait_send()
    if ny > 1:
        for j in rels:
            wy(j, 1).wait_send()
            wy(j, -1).wait_send()
            wy2(j).wait_send()
    for r in range(CHUNKS):
        scopy(0, h, r).wait_send()
        if nx > 1:
            xcopy(0, h, r, (c, hat(1))).wait_send()
            xcopy(1, h, r, (c, hat(-1))).wait_send()
            if r < half:
                xcopy(2, hat(-1), r, (c, hat(1))).wait_send()
            else:
                xcopy(2, hat(1), r, (c, hat(-1))).wait_send()
            scopy(1, hat(-1), r).wait_send()
            scopy(2, hat(1), r).wait_send()
            scopy(3, hat(2), r).wait_send()


def local(nz, ny, nx, queries, keys, values, input_pre, forget_pre, output_pre, w_out):
    tok, dk = queries.shape
    dv = values.shape[1]
    nh = 2 * nx
    qr = dk // ny
    tpo = (qr // 16) * (dv // 128) // nz
    dma = pltpu.SemaphoreType.DMA
    v = pltpu.VMEM
    y1, z1 = max(ny - 1, 1), max(nz - 1, 1)
    scratch = [
        v((ny, qr, dv), BF16), v((ny, qr, dv), BF16), v((ny, 8, 128), F32),
        v((nz, tpo * 16, 128), BF16), v((8, 128), F32),
        v((nz, tpo * 16, 128), BF16), v((nz, 8, 128), F32),
        v((nz, tpo * 16, 128), BF16), v((nz, 8, 128), F32),
        v((nz, tpo * 16, 128), BF16), v((ny, qr, dv), BF16), v((ny, 8, 128), F32),
        v((dk, dv), BF16), v((nh, tok, dv), BF16), v((nh * dv, dv), BF16),
        v((tok, dv), F32), v((tok, 128), F32), v((tok, 128), F32),
        dma((y1,)), dma((y1,)), dma((y1,)), dma((y1,)),
        dma((z1,)), dma((z1,)), dma((z1,)), dma((z1,)), dma((z1,)), dma((z1,)),
        dma((y1,)), dma((y1,)),
        dma((nz,)), dma((nz,)), dma((nz,)), dma((nz,)),
        dma((nz,)), dma((nz,)), dma((nz,)), dma((nz,)), dma((nz,)), dma((nz,)),
        dma((3, CHUNKS)), dma((3, CHUNKS)), dma((4, CHUNKS)), dma((4, CHUNKS)),
    ]
    return pl.pallas_call(
        functools.partial(kernel, nz, ny, nx),
        out_shape=jax.ShapeDtypeStruct((tok, dv), BF16),
        in_specs=[pl.BlockSpec(memory_space=pltpu.VMEM)] * 7,
        out_specs=pl.BlockSpec(memory_space=pltpu.VMEM),
        scratch_shapes=scratch,
        compiler_params=pltpu.CompilerParams(
            collective_id=0, has_side_effects=True, vmem_limit_bytes=48 * 1024 * 1024),
        name="mlstm_layer",
    )(queries, keys, values, input_pre.reshape(1, tok), forget_pre.reshape(1, tok),
      output_pre.reshape(1, tok), w_out)


def solution(mesh, ny=NY):
    nz = mesh.shape["ctx"] // ny
    nx = mesh.shape["head"] // 2
    spec = P("ctx", "head")
    return jax.shard_map(
        functools.partial(local, nz, ny, nx), mesh=mesh, in_specs=(spec,) * 7, out_specs=spec,
        check_vma=False)
```

time: 612 us -> 78.9 us (0.13)
  waiting for transfers between devices: 374 us -> 0 us
  blocking collectives: 196 us -> 0 us
  Pallas kernels: 0 us -> 71.7 us
  between operations: 13.2 us -> 0.02 us
  matrix products: 11.1 us -> 0 us
  other arithmetic: 7.88 us -> 0 us
    all_gather x3 -> x0, waiting for transfers between devices: 373 us -> none  [the longest x1 140 us: local(): gated_whole = lax.all_gather(gated_out, 'head', axis=1, tiled=True)]
    unnamed x1 -> x0, blocking collectives: 118 us -> none
    all_gather x1 -> x0, blocking collectives: 77.8 us -> none  [carried_in(): gathered = jax.tree.map(lambda a: lax.all_gather(a, axis), part)]
    pallas_call x0 -> x1, Pallas kernels: none -> 71.7 us  [local(): pl.pallas_call(functools.partial(kernel, nz, ny, nx), out_shape=jax.Shape...]
    dot_general x6 -> x0, matrix products: 11.1 us -> none  [the longest x1 6.59 us: local(): jnp.dot(gated_whole, lax.all_gather(w_out, 'ctx', axis=0, tiled=True), pr...]
  transfers between devices with their start and end apart: 3 -> 0, of which waited for: 3 -> 0; matrix products, arithmetic and copies ran while one was open for 1% -> 0% of each run, Pallas kernels for 0% -> 0%
where the time goes in v1:
time: 78.9 us; the launch traced here: 77.7 us
  Pallas kernels  71.7 us (91%)
  local copies, waits for them, and re-layouts  5.95 us (8%)
    pallas_call x1, Pallas kernels, local(): pl.pallas_call(functools.partial(kernel, nz, ny, nx), out_shape=jax.Shape...  71.7 us
    unnamed x15, local copies, waits for them, and re-layouts  5.95 us

profile of v1, /device:TPU:1, one launch (start us, length us, event | category | flops | bytes accessed | tf_op | source)
XLA Modules:
  0.0 77.7 jit_solution(14083677020353430440)
XLA Ops:
  0.0 0.0 copy-start.5
  0.0 0.0 copy-start.4
  0.0 0.7 copy-done.5
  0.7 0.0 copy-done.4
  0.7 0.0 copy-start
  0.7 1.0 %copy-done = bf16[512,512]{1,0:T(8,128)(2,1)S(1)} copy-done((bf16[512,512]{1,0:T(8,128)(2,1)S(1)}, bf16[512,512]{1,0:T(8,128)(2,1)}, u32[]{:S(2)}) %copy-start) | copy-done | bytes 524312
  1.7 0.0 copy-start.1
  1.7 0.9 %copy-done.1 = bf16[512,256]{1,0:T(8,128)(2,1)S(1)} copy-done((bf16[512,256]{1,0:T(8,128)(2,1)S(1)}, bf16[512,256]{1,0:T(8,128)(2,1)}, u32[]{:S(2)}) %copy-start.1) | copy-done | bytes 262168
  2.7 0.0 copy-start.2
  2.7 0.9 %copy-done.2 = bf16[512,256]{1,0:T(8,128)(2,1)S(1)} copy-done((bf16[512,256]{1,0:T(8,128)(2,1)S(1)}, bf16[512,256]{1,0:T(8,128)(2,1)}, u32[]{:S(2)}) %copy-start.2) | copy-done | bytes 262168
  3.6 0.0 copy-start.3
  3.6 0.8 %copy-done.3 = bf16[64,512]{1,0:T(8,128)(2,1)S(1)} copy-done((bf16[64,512]{1,0:T(8,128)(2,1)S(1)}, bf16[64,512]{1,0:T(8,128)(2,1)}, u32[]{:S(2)}) %copy-start.3) | copy-done | bytes 65560
  4.5 0.0 copy-start.6
  4.5 0.7 copy-done.6
  5.2 71.7 %mlstm_layer.1 = bf16[512,512]{1,0:T(8,128)(2,1)S(1)} custom-call(bf16[512,256]{1,0:T(8,128)(2,1)S(1)} %copy-done.1, bf16[512,256]{1,0:T(8,128)(2,1)S(1)} %copy-done.2, bf16[512,512]{1,0:T(8,128)(2,1)S(1)} %copy-done, f32[1,512]{1,0:T(1,128)S(1)} %bitcast.3, f32[1,512]{1,0:T(1,128)S(1)} %bitcast.4, f32[1,512]{1,0:T(1,128)S(1)} %bitcast.5, ...), custom_call_target="tpu_custom_call" | custom-call | tf_op jit(solution)/shard_map/mlstm_layer/pallas_call | solution.py:470
  76.9 0.8 %copy.9 = bf16[512,512]{1,0:T(8,128)(2,1)} copy(bf16[512,512]{1,0:T(8,128)(2,1)S(1)} %mlstm_layer.1) | data formatting | bytes 1048576
Async XLA Ops:
  0.0 0.7 copy-start.5
  0.0 0.7 copy-start.4
  0.7 1.0 %copy-start = (bf16[512,512]{1,0:T(8,128)(2,1)S(1)}, bf16[512,512]{1,0:T(8,128)(2,1)}, u32[]{:S(2)}) copy-start(bf16[512,512]{1,0:T(8,128)(2,1)} %v_ref.1) | copy-start | bytes 1572868
  1.7 0.9 %copy-start.1 = (bf16[512,256]{1,0:T(8,128)(2,1)S(1)}, bf16[512,256]{1,0:T(8,128)(2,1)}, u32[]{:S(2)}) copy-start(bf16[512,256]{1,0:T(8,128)(2,1)} %q_ref.1) | copy-start | bytes 786436
  2.7 0.9 %copy-start.2 = (bf16[512,256]{1,0:T(8,128)(2,1)S(1)}, bf16[512,256]{1,0:T(8,128)(2,1)}, u32[]{:S(2)}) copy-start(bf16[512,256]{1,0:T(8,128)(2,1)} %k_ref.1) | copy-start | bytes 786436
  3.6 0.8 %copy-start.3 = (bf16[64,512]{1,0:T(8,128)(2,1)S(1)}, bf16[64,512]{1,0:T(8,128)(2,1)}, u32[]{:S(2)}) copy-start(bf16[64,512]{1,0:T(8,128)(2,1)} %w_ref.1) | copy-start | bytes 196612
  4.5 0.7 copy-start.6

commit v2 on v1

v2 whole, which is shorter than its diff:
```python
import functools

import jax
import jax.numpy as jnp
from jax import lax
from jax.experimental import pallas as pl
from jax.experimental.pallas import tpu as pltpu
from jax.sharding import PartitionSpec as P

MESH = pl.DeviceIdType.MESH
F32 = jnp.float32
BF16 = jnp.bfloat16
NY = 4


def _log_sigmoid(f):
    e = jnp.exp(-jnp.abs(f))
    s = e / (2.0 + e)
    s2 = s * s
    poly = jnp.full_like(s, 1.0 / 15.0)
    for d in (13.0, 11.0, 9.0, 7.0, 5.0, 3.0, 1.0):
        poly = poly * s2 + 1.0 / d
    return jnp.minimum(f, 0.0) - 2.0 * s * poly


def _combine_top(top, decay, fresh):
    new = jnp.maximum(decay + top, fresh)
    return new, jnp.exp(decay + top - new), jnp.exp(fresh - new)


def _wide(row, n):
    return jnp.concatenate([row] * n, axis=1)


class Sems:
    def __init__(self, name, ref):
        self.name, self.ref = name, ref

    def __call__(self, *index):
        return (self.name,) + index, self.ref.at[index if len(index) > 1 else index[0]]


def kernel(nz, ny, nx, q_hbm, k_hbm, v_hbm, i_hbm, f_hbm, o_hbm, w_hbm, out_ref, *scr):
    (k_ref, v_ref, i_ref, f_ref, o_ref, ins, mloc, ybuf, sy, tt, stt, ta, sta, pb, sp, pz, mo, sm, cols,
     qbuf, nbuf, mbuf, cbuf, gbuf, wa, wb, *sems) = scr
    (s1s, s1r, s1bs, s1br, s3s, s3r, s3bs, s3br, s5s, s5r, s6s, s6r, wafs, wafr, wabs, wabr,
     wbfs, wbfr, wbbs, wbbr, w0s, w0r, yps, ypr, yms, ymr, y2s, y2r, xs, xr, bs, br, cs, cr) = [
        Sems(n, ref) for n, ref in enumerate(sems)]
    tok, dk = k_ref.shape
    dv = v_ref.shape[1]
    wr = w_hbm.shape[0]
    wc = dv // 2
    nh = 2 * nx
    qr = dk // ny
    lt = dv // 128
    nt = (qr // 16) * lt
    tpo = nt // nz
    scale = dk ** (-0.5)
    c = lax.axis_index("ctx")
    h = lax.axis_index("head")
    z, y = lax.div(c, ny), lax.rem(c, ny)
    x, core = lax.div(h, 2), lax.rem(h, 2)
    sib = h + 1 - 2 * core

    def wpiece(buf, dz, dy):
        row = pl.multiple_of((zat(dz) * ny + yat(dy)) * wr, wr)
        return buf.at[pl.ds(row, wr), :]

    def zat(d):
        return lax.rem(z + (d + nz), nz)

    def yat(d):
        return lax.rem(y + (d + ny), ny)

    def hat(d, other=0):
        side = 1 - core if other else core
        return lax.rem(x + (d + nx), nx) * 2 + side

    def dev(zz, yy, hh):
        return (zz * ny + yy, hh)

    loads = [
        pltpu.make_async_copy(src, dst, ins.at[n]) for n, (src, dst) in enumerate((
            (f_hbm, f_ref), (i_hbm, i_ref), (o_hbm, o_ref), (k_hbm, k_ref), (v_hbm, v_ref),
            (q_hbm, qbuf.at[h]),
            (w_hbm.at[:, 0:wc], wpiece(wa, 0, 0)), (w_hbm.at[:, wc:dv], wpiece(wb, 0, 0))))
    ]
    for load in loads:
        load.start()

    started, got = {}, set()

    def send(src, dst, ss, rs, to):
        copy = pltpu.make_async_remote_copy(
            src_ref=src, dst_ref=dst, send_sem=ss[1], recv_sem=rs[1], device_id=to, device_id_type=MESH)
        started[rs[0]] = copy
        copy.start()

    def take(rs):
        got.add(rs[0])
        started[rs[0]].wait_recv()

    partners = [dev(z, yat(d), h) for d in range(1, ny)]
    partners += [dev(zat(d), y, h) for d in range(1, nz)]
    partners += [(c, lax.rem(h + d, nh)) for d in range(1, nh)]
    barrier = pltpu.get_barrier_semaphore()
    for p in partners:
        pl.semaphore_signal(barrier, inc=1, device_id=p, device_id_type=MESH)

    nf = nz // 2
    nb = nz - 1 - nf
    rels = list(range(-nf, nb + 1))
    half_plane = ny * wr // 2

    def plane(dz, part):
        row = pl.multiple_of(zat(dz) * (ny * wr) + part * half_plane, half_plane)
        return wb.at[pl.ds(row, half_plane), :]

    def wa_send(step, sign):
        piece = wpiece(wa, -sign * (step - 1), 0)
        ss, rs = (wafs, wafr) if sign > 0 else (wabs, wabr)
        send(piece, piece, ss(step - 1), rs(step - 1), dev(zat(sign), y, h))

    def wb_send(step, sign, part):
        piece = plane(-sign * (step - 1), part)
        ss, rs = (wbfs, wbfr) if sign > 0 else (wbbs, wbbr)
        send(piece, piece, ss(step - 1, part), rs(step - 1, part), dev(zat(sign), y, h))

    ways = ((1, nf, wafr, wbfr), (-1, nb, wabr, wbbr))

    def wa_step(step):
        for sign, last, ra, _ in ways:
            if 1 <= step <= last:
                take(ra(step - 1))
            if step + 1 <= last:
                wa_send(step + 1, sign)

    def wb_step(step):
        for part in (0, 1):
            for sign, last, _, rb in ways:
                if 1 <= step <= last:
                    take(rb(step - 1, part))
                if step + 1 <= last:
                    wb_send(step + 1, sign, part)

    def wb_first():
        for d in range(1, ny):
            piece = wpiece(wb, 0, 0)
            send(piece, piece, w0s(d - 1), w0r(d - 1), dev(z, yat(d), h))

    def wb_row():
        for d in range(1, ny):
            take(w0r(d - 1))
        wb_step(0)

    def wa_across(*js):
        for j in js:
            if ny > 1 and j in rels:
                piece = wpiece(wa, j, 0)
                send(piece, piece, yps(j + nf), ypr(j + nf), dev(z, yat(1), h))
                send(piece, piece, yms(j + nf), ymr(j + nf), dev(z, yat(-1), h))

    def wa_relay(*js):
        for j in js:
            if ny > 1 and j in rels:
                take(ypr(j + nf))
                take(ymr(j + nf))
                sign = 1 if j % 2 == 0 else -1
                piece = wpiece(wa, j, -sign)
                send(piece, piece, y2s(j + nf), y2r(j + nf), dev(z, yat(sign), h))

    def item(n, hh):
        if n < 2:
            return qbuf.at[hh, pl.ds(n * (tok // 2), tok // 2), :]
        if n < 6:
            return nbuf.at[hh, pl.ds((n - 2) * (tok // 4), tok // 4), :]
        return mbuf.at[hh, pl.ds(pl.multiple_of(yat(6 - n) * qr, qr), qr), :]

    def onward(n):
        return 1 if n in (0, 2, 3, 6, 7) else -1

    def x_side(n, slot, hh):
        piece = item(n, hh)
        send(piece, piece, bs(slot, n), br(slot, n), (c, sib))

    def x_send(n):
        piece = item(n, h)
        if nx > 1:
            send(piece, piece, xs(0, n), xr(0, n), (c, hat(1)))
            send(piece, piece, xs(1, n), xr(1, n), (c, hat(-1)))
        x_side(n, 0, h)

    def x_relay(n):
        if nx > 1:
            for slot, d in ((0, -1), (1, 1)):
                take(xr(slot, n))
                if onward(n) == -d:
                    piece = item(n, hat(d))
                    send(piece, piece, xs(2, n), xr(2, n), (c, hat(-d)))
                x_side(n, 1 + slot, hat(d))

    def x_last(n):
        if nx > 1:
            take(xr(2, n))
            x_side(n, 3, hat(2))

    for load in loads[0:3]:
        load.wait()
    lane = lax.broadcasted_iota(jnp.int32, (8, tok), 1)
    gate_in = jnp.broadcast_to(i_ref[...], (8, tok))
    cum = _log_sigmoid(jnp.broadcast_to(f_ref[...], (8, tok)))
    sh = 1
    while sh < tok:
        cum = cum + jnp.where(lane >= sh, pltpu.roll(cum, sh, 1), 0.0)
        sh *= 2
    a_row = gate_in - cum
    top_row = a_row
    sh = 1
    while sh < tok:
        top_row = jnp.maximum(top_row, jnp.where(lane >= sh, pltpu.roll(top_row, sh, 1), -3e38))
        sh *= 2
    sig = 1.0 / (1.0 + jnp.exp(-jnp.broadcast_to(o_ref[...], (8, tok))))
    decay = cum[0:1, tok - 1:tok]
    a_last = top_row[0:1, tok - 1:tok]
    kw_row = jnp.exp(a_row - a_last)
    rows = lax.broadcasted_iota(jnp.int32, (128, tok), 0)
    stack = jnp.where(rows == 0, top_row[0:1], jnp.where(rows == 1, cum[0:1],
            jnp.where(rows == 2, sig[0:1], kw_row[0:1])))
    cols[...] = jnp.transpose(stack)
    a1 = a_row[0:1]

    loads[3].wait()
    loads[4].wait()
    scaled = k_ref[...].astype(F32) * cols[:, 3:4]
    norm = jnp.sum(scaled, axis=0, keepdims=True)
    m_local = lax.dot_general(
        scaled.astype(BF16), v_ref[...], (((0,), (0,)), ((), ())), preferred_element_type=F32
    )
    for j in range(ny):
        mloc[j] = m_local[j * qr:(j + 1) * qr].astype(BF16)
    pad = [jnp.zeros((4, 128), F32)]
    stat = jnp.concatenate(
        [norm[:, 0:128], norm[:, 128:256], jnp.broadcast_to(decay, (1, 128)),
         jnp.broadcast_to(decay + a_last, (1, 128))] + pad, axis=0)
    sy[y] = stat
    ybuf[y] = mloc[y]
    for load in loads[5:]:
        load.wait()

    pl.semaphore_wait(barrier, len(partners))

    for d in range(1, ny):
        to = dev(z, yat(d), h)
        send(sy.at[y], sy.at[y], s1bs(d - 1), s1br(d - 1), to)
        send(mloc.at[yat(d)], ybuf.at[y], s1s(d - 1), s1r(d - 1), to)
    wb_first()
    wa_step(0)
    x_send(0)
    x_send(1)

    rb = tok // 4
    dens = []
    for r in range(4):
        width = (r + 1) * rb
        sl = pl.ds(r * rb, rb)
        scores = lax.dot_general(
            qbuf[h, sl, :], k_ref[0:width, :], (((1,), (1,)), ((), ())), preferred_element_type=F32
        ) * scale
        ti = lax.broadcasted_iota(jnp.int32, (rb, width), 0) + r * rb
        si = lax.broadcasted_iota(jnp.int32, (rb, width), 1)
        rel = jnp.where(ti >= si, a1[:, 0:width] - cols[sl, 0:1], -1e30)
        weighted = jnp.exp(rel) * scores
        dens.append(jnp.sum(weighted, axis=1, keepdims=True))
        nbuf[h, sl, :] = jnp.dot(
            weighted.astype(BF16), v_ref[0:width, :], preferred_element_type=F32).astype(BF16)
        x_send(2 + r)
    den_loc = jnp.concatenate(dens, axis=0)

    for d in range(1, ny):
        take(s1br(d - 1))
        take(s1r(d - 1))
    dec = [sy[j, 2:3, :] for j in range(ny)]
    tops = [sy[j, 3:4, :] for j in range(ny)]
    suffix = jnp.zeros((1, 128), F32)
    logs = [None] * ny
    for j in reversed(range(ny)):
        logs[j] = suffix + tops[j]
        suffix = suffix + dec[j]
    top_t = functools.reduce(jnp.maximum, logs)
    wts = [jnp.exp(lg - top_t) for lg in logs]
    total = sum(_wide(wts[j], lt) * ybuf[j].astype(F32) for j in range(ny))
    for t in range(nt):
        a, b = divmod(t, lt)
        o, s = divmod(t, tpo)
        tt[o, s * 16:(s + 1) * 16, :] = total[a * 16:(a + 1) * 16, b * 128:(b + 1) * 128].astype(BF16)
    norm_t = sum(wts[j] * sy[j, 0:2, :] for j in range(ny))
    stt[...] = jnp.concatenate([norm_t, suffix, top_t] + pad, axis=0)
    ta[z] = tt[z]
    sta[z] = stt[...]

    far = sorted(range(1, nz), key=lambda d: -min(d, nz - d))
    for d in far:
        to = dev(zat(d), y, h)
        send(stt, sta.at[z], s3bs(d - 1), s3br(d - 1), to)
        send(tt.at[zat(d)], ta.at[z], s3s(d - 1), s3r(d - 1), to)

    wa_across(0)
    wb_row()
    wa_step(1)
    wa_across(-1, 1)
    x_relay(0)
    x_relay(1)
    wb_step(1)
    wa_step(2)

    for d in far:
        take(s3br(d - 1))
        take(s3r(d - 1))
    state = jnp.zeros((tpo * 16, 128), F32)
    norm_p = jnp.zeros((2, 128), F32)
    top_p = jnp.full((1, 128), -1e30, F32)
    for zz in range(nz):
        pb[zz] = state.astype(BF16)
        sp[zz, 0:2, :] = norm_p
        sp[zz, 2:3, :] = top_p
        if zz + 1 < nz:
            top_p, keep, fresh = _combine_top(top_p, sta[zz, 2:3, :], sta[zz, 3:4, :])
            state = keep * state + fresh * ta[zz].astype(F32)
            norm_p = keep * norm_p + fresh * sta[zz, 0:2, :]
    pz[z] = pb[z]
    for d in far:
        send(pb.at[zat(d)], pz.at[z], s5s(d - 1), s5r(d - 1), dev(zat(d), y, h))

    wa_across(-2, 2)
    wb_step(2)
    wa_step(3)

    norm_p = sp[z, 0:2, :]
    top_p = sp[z, 2:3, :]
    keeps, freshs = [], []
    for j in range(ny):
        sm[j, 0:2, :] = norm_p
        sm[j, 2:3, :] = top_p
        if j + 1 < ny:
            top_p, keep, fresh = _combine_top(top_p, dec[j], tops[j])
            keeps.append(keep)
            freshs.append(fresh)
            norm_p = keep * norm_p + fresh * sy[j, 0:2, :]
    norm_prev = sm[y, 0:2, :]
    top_prev = sm[y, 2:3, :][:, 0:1]
    norm_row = jnp.concatenate([norm_prev[0:1], norm_prev[1:2]], axis=1)
    q_norm = jnp.sum(qbuf[h].astype(F32) * norm_row, axis=1, keepdims=True) * scale
    top_loc = cols[:, 0:1]
    top_mix = jnp.maximum(top_loc, top_prev)
    inner = jnp.exp(top_loc - top_mix)
    lift = jnp.exp(top_prev - top_mix)
    den = jnp.maximum(
        jnp.abs(inner * den_loc + lift * q_norm), jnp.exp(-(cols[:, 1:2] + top_mix)))
    gate = cols[:, 2:3] / den
    which = lax.broadcasted_iota(jnp.int32, (tok, 128), 1)
    both = jnp.where(which == 0, gate * inner, gate * (lift * scale))
    cbuf[h] = jnp.transpose(both)[0:8, :]
    for d in range(1, nh):
        send(cbuf.at[h], cbuf.at[h], cs(d - 1), cr(d - 1), (c, lax.rem(h + d, nh)))

    x_relay(2)
    wa_across(-3, 3)
    wa_relay(0)
    wb_step(3)
    wa_step(4)
    x_relay(3)

    for d in far:
        take(s5r(d - 1))
    tiles = [pz[t // tpo, (t % tpo) * 16:(t % tpo + 1) * 16, :].astype(F32) for t in range(nt)]
    state = jnp.concatenate(
        [jnp.concatenate(tiles[a * lt:(a + 1) * lt], axis=1) for a in range(qr // 16)], axis=0)
    for j in range(ny):
        mo[j] = state.astype(BF16)
        if j + 1 < ny:
            state = _wide(keeps[j], lt) * state + _wide(freshs[j], lt) * ybuf[j].astype(F32)
    own_quarter = pl.ds(pl.multiple_of(y * qr, qr), qr)
    mbuf[h, own_quarter, :] = mo[y]
    for d in range(1, ny):
        send(mo.at[yat(d)], mbuf.at[h, own_quarter, :], s6s(d - 1), s6r(d - 1), dev(z, yat(d), h))
    x_send(6)

    wb_step(4)
    wa_step(5)
    wa_across(-4, 4)
    wa_relay(-1, 1)
    x_relay(4)
    wb_step(5)
    wa_step(6)
    x_relay(5)

    for d in sorted(range(1, ny), key=lambda d: min(d, ny - d)):
        take(s6r(d - 1))
        x_send(6 + d)
    for n in range(2, 6):
        x_last(n)
    x_last(0)
    x_last(1)
    wa_across(-5, 5, -6, 6)
    wa_relay(-2, 2)
    wb_step(6)
    wa_step(7)
    wa_across(-7, 7)
    x_relay(6)
    wa_relay(-3, 3)
    order = [6] + [6 + d for d in sorted(range(1, ny), key=lambda d: min(d, ny - d))]
    wb_step(7)
    wa_step(8)
    wa_across(-8)
    for n in order[1:]:
        x_relay(n)
    wb_step(8)
    wa_relay(-4, 4, -5, 5)
    for n in order:
        x_last(n)
    wa_relay(-6, 6, -7, 7, -8)

    for d in range(1, nh):
        take(cr(d - 1))
    heads = [(0, h, None), (1, sib, 0)]
    if nx > 1:
        heads += [(2, hat(-1), None), (3, hat(-1, 1), 1), (4, hat(1), None), (5, hat(1, 1), 2),
                  (6, hat(2), None), (7, hat(2, 1), 3)]
    factors = [cbuf[hh] for _, hh, _ in heads]
    if nh < 16:
        factors += [jnp.zeros((128 - 8 * nh, tok), F32)]
    cols[...] = jnp.transpose(jnp.concatenate(factors, axis=0))
    items = range(6 + ny)
    for n, hh, slot in heads:
        if slot is not None:
            for m in items:
                take(br(slot, m))
        for r in range(2):
            sl = pl.ds(r * (tok // 2), tok // 2)
            far_part = jnp.dot(qbuf[hh, sl, :], mbuf[hh], preferred_element_type=F32)
            near = nbuf[hh, sl, :].astype(F32)
            gbuf[hh, sl, :] = (
                cols[sl, 8 * n:8 * n + 1] * near + cols[sl, 8 * n + 1:8 * n + 2] * far_part
            ).astype(BF16)

    if ny > 1:
        for j in rels:
            take(y2r(j + nf))

    for rr in range(tok // 256):
        sl = slice(rr * 256, (rr + 1) * 256)
        for buf, col in ((wa, 0), (wb, wc)):
            acc = jnp.zeros((256, wc), F32)
            for hh in range(nh):
                acc = acc + jnp.dot(
                    gbuf[hh, sl, :], buf[hh * dv:(hh + 1) * dv, :], preferred_element_type=F32)
            out_ref[sl, col:col + wc] = acc.astype(BF16)

    assert set(started) == got
    for copy in started.values():
        copy.wait_send()


def local(nz, ny, nx, queries, keys, values, input_pre, forget_pre, output_pre, w_out):
    tok, dk = queries.shape
    dv = values.shape[1]
    nh = 2 * nx
    qr = dk // ny
    tpo = (qr // 16) * (dv // 128) // nz
    v = pltpu.VMEM
    y1, z1 = max(ny - 1, 1), max(nz - 1, 1)
    items = 6 + ny
    scratch = [
        v((tok, dk), BF16), v((tok, dv), BF16), v((1, tok), F32), v((1, tok), F32), v((1, tok), F32),
        pltpu.SemaphoreType.DMA((8,)),
        v((ny, qr, dv), BF16), v((ny, qr, dv), BF16), v((ny, 8, 128), F32),
        v((nz, tpo * 16, 128), BF16), v((8, 128), F32),
        v((nz, tpo * 16, 128), BF16), v((nz, 8, 128), F32),
        v((nz, tpo * 16, 128), BF16), v((nz, 8, 128), F32),
        v((nz, tpo * 16, 128), BF16), v((ny, qr, dv), BF16), v((ny, 8, 128), F32),
        v((tok, 128), F32),
        v((nh, tok, dk), BF16), v((nh, tok, dv), BF16), v((nh, dk, dv), BF16), v((nh, 8, tok), F32),
        v((nh, tok, dv), BF16), v((nh * dv, dv // 2), BF16), v((nh * dv, dv // 2), BF16),
    ]
    counts = [(y1,)] * 4 + [(z1,)] * 6 + [(y1,)] * 2 + [(nz,)] * 4 + [(nz, 2)] * 4 + [(y1,)] * 2
    counts += [(nz,)] * 6 + [(3, items)] * 2 + [(4, items)] * 2 + [(nh,)] * 2
    scratch += [pltpu.SemaphoreType.DMA(n) for n in counts]
    return pl.pallas_call(
        functools.partial(kernel, nz, ny, nx),
        out_shape=jax.ShapeDtypeStruct((tok, dv), BF16),
        in_specs=[pl.BlockSpec(memory_space=pl.ANY)] * 7,
        out_specs=pl.BlockSpec(memory_space=pltpu.VMEM),
        scratch_shapes=scratch,
        compiler_params=pltpu.CompilerParams(
            collective_id=0, has_side_effects=True, vmem_limit_bytes=60 * 1024 * 1024),
        name="mlstm_layer",
    )(queries, keys, values, input_pre.reshape(1, tok), forget_pre.reshape(1, tok),
      output_pre.reshape(1, tok), w_out)


def solution(mesh, ny=NY):
    nz = mesh.shape["ctx"] // ny
    nx = mesh.shape["head"] // 2
    spec = P("ctx", "head")
    return jax.shard_map(
        functools.partial(local, nz, ny, nx), mesh=mesh, in_specs=(spec,) * 7, out_specs=spec,
        check_vma=False)
```

time: 78.9 us -> 78.6 us (level)
  Pallas kernels: 71.7 us -> 76 us
  local copies, waits for them, and re-layouts: 5.95 us -> 1.87 us
    pallas_call x1, Pallas kernels: 71.7 us -> 76 us  [local(): pl.pallas_call(functools.partial(kernel, nz, ny, nx), out_shape=jax.Shape...]
    unnamed x15 -> x1, local copies, waits for them, and re-layouts: 5.95 us -> 1.87 us
where the time goes in v2:
time: 78.6 us; the launch traced here: 77.9 us
  Pallas kernels  76 us (97%)
  local copies, waits for them, and re-layouts  1.87 us (2%)
    pallas_call x1, Pallas kernels, local(): pl.pallas_call(functools.partial(kernel, nz, ny, nx), out_shape=jax.Shape...  76 us
    unnamed x1, local copies, waits for them, and re-layouts  1.87 us

profile of v2, /device:TPU:1, one launch (start us, length us, event | category | flops | bytes accessed | tf_op | source)
XLA Modules:
  0.0 77.9 jit_solution(2622763474148276519)
XLA Ops:
  0.0 76.0 %mlstm_layer.1 = bf16[512,512]{1,0:T(8,128)(2,1)} custom-call(bf16[512,256]{1,0:T(8,128)(2,1)} %q_hbm.1, bf16[512,256]{1,0:T(8,128)(2,1)} %k_hbm.1, bf16[512,512]{1,0:T(8,128)(2,1)} %v_hbm.1, f32[1,512]{1,0:T(1,128)} %bitcast.3, f32[1,512]{1,0:T(1,128)} %bitcast.4, f32[1,512]{1,0:T(1,128)} %bitcast.5, bf16[64,512]{1,0:T(8,128)(2,1)} %w_hbm.1), custom_call_target="tpu_custom_call" | custom-call | tf_op jit(solution)/shard_map/mlstm_layer/pallas_call | solution.py:488
  76.0 1.9 %copy.9 = bf16[512,512]{1,0:T(8,128)(2,1)} copy(bf16[512,512]{1,0:T(8,128)(2,1)} %mlstm_layer.1) | data formatting | bytes 1048576

commit v3 on v2

--- a/solution.py
+++ b/solution.py
@@ -42,14 +42,15 @@
 
 def kernel(nz, ny, nx, q_hbm, k_hbm, v_hbm, i_hbm, f_hbm, o_hbm, w_hbm, out_ref, *scr):
     (k_ref, v_ref, i_ref, f_ref, o_ref, ins, mloc, ybuf, sy, tt, stt, ta, sta, pb, sp, pz, mo, sm, cols,
-     qbuf, nbuf, mbuf, cbuf, gbuf, wa, wb, *sems) = scr
+     qbuf, nbuf, mbuf, cbuf, gbuf, wbuf, *sems) = scr
     (s1s, s1r, s1bs, s1br, s3s, s3r, s3bs, s3br, s5s, s5r, s6s, s6r, wafs, wafr, wabs, wabr,
      wbfs, wbfr, wbbs, wbbr, w0s, w0r, yps, ypr, yms, ymr, y2s, y2r, xs, xr, bs, br, cs, cr) = [
         Sems(n, ref) for n, ref in enumerate(sems)]
     tok, dk = k_ref.shape
     dv = v_ref.shape[1]
     wr = w_hbm.shape[0]
-    wc = dv // 2
+    wa_rows = 3 * wr // 4
+    parts = 2 if ny > 1 else 1
     nh = 2 * nx
     qr = dk // ny
     lt = dv // 128
@@ -62,9 +63,11 @@
     x, core = lax.div(h, 2), lax.rem(h, 2)
     sib = h + 1 - 2 * core
 
-    def wpiece(buf, dz, dy):
-        row = pl.multiple_of((zat(dz) * ny + yat(dy)) * wr, wr)
-        return buf.at[pl.ds(row, wr), :]
+    def wa_piece(dz, dy):
+        return wbuf.at[zat(dz) * ny + yat(dy), 0:wa_rows, :]
+
+    def wb_piece():
+        return wbuf.at[c, wa_rows:wr, :]
 
     def zat(d):
         return lax.rem(z + (d + nz), nz)
@@ -81,9 +84,8 @@
 
     loads = [
         pltpu.make_async_copy(src, dst, ins.at[n]) for n, (src, dst) in enumerate((
-            (f_hbm, f_ref), (i_hbm, i_ref), (o_hbm, o_ref), (k_hbm, k_ref), (v_hbm, v_ref),
-            (q_hbm, qbuf.at[h]),
-            (w_hbm.at[:, 0:wc], wpiece(wa, 0, 0)), (w_hbm.at[:, wc:dv], wpiece(wb, 0, 0))))
+            (f_hbm, f_ref), (i_hbm, i_ref), (o_hbm, o_ref), (w_hbm, wbuf.at[c]),
+            (q_hbm, qbuf.at[h]), (k_hbm, k_ref), (v_hbm, v_ref)))
     ]
     for load in loads:
         load.start()
@@ -110,14 +112,12 @@
     nf = nz // 2
     nb = nz - 1 - nf
     rels = list(range(-nf, nb + 1))
-    half_plane = ny * wr // 2
 
     def plane(dz, part):
-        row = pl.multiple_of(zat(dz) * (ny * wr) + part * half_plane, half_plane)
-        return wb.at[pl.ds(row, half_plane), :]
+        return wbuf.at[pl.ds(zat(dz) * ny + part * (ny // parts), ny // parts), wa_rows:wr, :]
 
     def wa_send(step, sign):
-        piece = wpiece(wa, -sign * (step - 1), 0)
+        piece = wa_piece(-sign * (step - 1), 0)
         ss, rs = (wafs, wafr) if sign > 0 else (wabs, wabr)
         send(piece, piece, ss(step - 1), rs(step - 1), dev(zat(sign), y, h))
 
@@ -136,7 +136,7 @@
                 wa_send(step + 1, sign)
 
     def wb_step(step):
-        for part in (0, 1):
+        for part in range(parts):
             for sign, last, _, rb in ways:
                 if 1 <= step <= last:
                     take(rb(step - 1, part))
@@ -145,7 +145,7 @@
 
     def wb_first():
         for d in range(1, ny):
-            piece = wpiece(wb, 0, 0)
+            piece = wb_piece()
             send(piece, piece, w0s(d - 1), w0r(d - 1), dev(z, yat(d), h))
 
     def wb_row():
@@ -156,7 +156,7 @@
     def wa_across(*js):
         for j in js:
             if ny > 1 and j in rels:
-                piece = wpiece(wa, j, 0)
+                piece = wa_piece(j, 0)
                 send(piece, piece, yps(j + nf), ypr(j + nf), dev(z, yat(1), h))
                 send(piece, piece, yms(j + nf), ymr(j + nf), dev(z, yat(-1), h))
 
@@ -166,7 +166,7 @@
                 take(ypr(j + nf))
                 take(ymr(j + nf))
                 sign = 1 if j % 2 == 0 else -1
-                piece = wpiece(wa, j, -sign)
+                piece = wa_piece(j, -sign)
                 send(piece, piece, y2s(j + nf), y2r(j + nf), dev(z, yat(sign), h))
 
     def item(n, hh):
@@ -228,9 +228,18 @@
             jnp.where(rows == 2, sig[0:1], kw_row[0:1])))
     cols[...] = jnp.transpose(stack)
     a1 = a_row[0:1]
-
     loads[3].wait()
     loads[4].wait()
+
+    pl.semaphore_wait(barrier, len(partners))
+    wa_step(0)
+    wb_first()
+    x_send(0)
+    x_send(1)
+    wa_across(0)
+
+    loads[5].wait()
+    loads[6].wait()
     scaled = k_ref[...].astype(F32) * cols[:, 3:4]
     norm = jnp.sum(scaled, axis=0, keepdims=True)
     m_local = lax.dot_general(
@@ -244,19 +253,12 @@
          jnp.broadcast_to(decay + a_last, (1, 128))] + pad, axis=0)
     sy[y] = stat
     ybuf[y] = mloc[y]
-    for load in loads[5:]:
-        load.wait()
-
-    pl.semaphore_wait(barrier, len(partners))
-
     for d in range(1, ny):
         to = dev(z, yat(d), h)
         send(sy.at[y], sy.at[y], s1bs(d - 1), s1br(d - 1), to)
         send(mloc.at[yat(d)], ybuf.at[y], s1s(d - 1), s1r(d - 1), to)
-    wb_first()
-    wa_step(0)
-    x_send(0)
-    x_send(1)
+    wb_row()
+    wa_step(1)
 
     rb = tok // 4
     dens = []
@@ -304,14 +306,16 @@
         send(stt, sta.at[z], s3bs(d - 1), s3br(d - 1), to)
         send(tt.at[zat(d)], ta.at[z], s3s(d - 1), s3r(d - 1), to)
 
-    wa_across(0)
-    wb_row()
-    wa_step(1)
-    wa_across(-1, 1)
+    wb_step(1)
+    wa_step(2)
+    wa_across(-1, 1, -2, 2)
     x_relay(0)
     x_relay(1)
-    wb_step(1)
-    wa_step(2)
+    wb_step(2)
+    wa_step(3)
+    wa_relay(0)
+    wb_step(3)
+    wa_step(4)
 
     for d in far:
         take(s3br(d - 1))
@@ -331,9 +335,10 @@
     for d in far:
         send(pb.at[zat(d)], pz.at[z], s5s(d - 1), s5r(d - 1), dev(zat(d), y, h))
 
-    wa_across(-2, 2)
-    wb_step(2)
-    wa_step(3)
+    wa_across(-3, 3)
+    x_relay(2)
+    wb_step(4)
+    wa_step(5)
 
     norm_p = sp[z, 0:2, :]
     top_p = sp[z, 2:3, :]
@@ -363,12 +368,11 @@
     for d in range(1, nh):
         send(cbuf.at[h], cbuf.at[h], cs(d - 1), cr(d - 1), (c, lax.rem(h + d, nh)))
 
-    x_relay(2)
-    wa_across(-3, 3)
-    wa_relay(0)
-    wb_step(3)
-    wa_step(4)
     x_relay(3)
+    wb_step(5)
+    wa_step(6)
+    wa_across(-4, 4)
+    wa_relay(-1, 1)
 
     for d in far:
         take(s5r(d - 1))
@@ -385,13 +389,9 @@
         send(mo.at[yat(d)], mbuf.at[h, own_quarter, :], s6s(d - 1), s6r(d - 1), dev(z, yat(d), h))
     x_send(6)
 
-    wb_step(4)
-    wa_step(5)
-    wa_across(-4, 4)
-    wa_relay(-1, 1)
+    wb_step(6)
+    wa_step(7)
     x_relay(4)
-    wb_step(5)
-    wa_step(6)
     x_relay(5)
 
     for d in sorted(range(1, ny), key=lambda d: min(d, ny - d)):
@@ -403,22 +403,18 @@
     x_last(1)
     wa_across(-5, 5, -6, 6)
     wa_relay(-2, 2)
-    wb_step(6)
-    wa_step(7)
-    wa_across(-7, 7)
-    x_relay(6)
+    wb_step(7)
+    wa_step(8)
+    wb_step(8)
+    wa_across(-7, 7, -8)
     wa_relay(-3, 3)
     order = [6] + [6 + d for d in sorted(range(1, ny), key=lambda d: min(d, ny - d))]
-    wb_step(7)
-    wa_step(8)
-    wa_across(-8)
-    for n in order[1:]:
+    for n, js in zip(order, ((-4, 4), (-5, 5), (-6, 6), (-7,))):
         x_relay(n)
-    wb_step(8)
-    wa_relay(-4, 4, -5, 5)
+        wa_relay(*js)
+    wa_relay(*((7, -8) if ny > 1 else ()))
     for n in order:
         x_last(n)
-    wa_relay(-6, 6, -7, 7, -8)
 
     for d in range(1, nh):
         take(cr(d - 1))
@@ -447,14 +443,17 @@
         for j in rels:
             take(y2r(j + nf))
 
+    if wr >= dv:
+        weights = [wbuf[hh * dv // wr, hh * dv % wr:hh * dv % wr + dv, :] for hh in range(nh)]
+    else:
+        per = dv // wr
+        weights = [wbuf[hh * per:(hh + 1) * per].reshape(dv, dv) for hh in range(nh)]
     for rr in range(tok // 256):
         sl = slice(rr * 256, (rr + 1) * 256)
-        for buf, col in ((wa, 0), (wb, wc)):
-            acc = jnp.zeros((256, wc), F32)
-            for hh in range(nh):
-                acc = acc + jnp.dot(
-                    gbuf[hh, sl, :], buf[hh * dv:(hh + 1) * dv, :], preferred_element_type=F32)
-            out_ref[sl, col:col + wc] = acc.astype(BF16)
+        acc = jnp.zeros((256, dv), F32)
+        for hh in range(nh):
+            acc = acc + jnp.dot(gbuf[hh, sl, :], weights[hh], preferred_element_type=F32)
+        out_ref[sl, :] = acc.astype(BF16)
 
     assert set(started) == got
     for copy in started.values():
@@ -472,7 +471,7 @@
     items = 6 + ny
     scratch = [
         v((tok, dk), BF16), v((tok, dv), BF16), v((1, tok), F32), v((1, tok), F32), v((1, tok), F32),
-        pltpu.SemaphoreType.DMA((8,)),
+        pltpu.SemaphoreType.DMA((7,)),
         v((ny, qr, dv), BF16), v((ny, qr, dv), BF16), v((ny, 8, 128), F32),
         v((nz, tpo * 16, 128), BF16), v((8, 128), F32),
         v((nz, tpo * 16, 128), BF16), v((nz, 8, 128), F32),
@@ -480,7 +479,7 @@
         v((nz, tpo * 16, 128), BF16), v((ny, qr, dv), BF16), v((ny, 8, 128), F32),
         v((tok, 128), F32),
         v((nh, tok, dk), BF16), v((nh, tok, dv), BF16), v((nh, dk, dv), BF16), v((nh, 8, tok), F32),
-        v((nh, tok, dv), BF16), v((nh * dv, dv // 2), BF16), v((nh * dv, dv // 2), BF16),
+        v((nh, tok, dv), BF16), v((nh * dv // w_out.shape[0],) + w_out.shape, BF16),
     ]
     counts = [(y1,)] * 4 + [(z1,)] * 6 + [(y1,)] * 2 + [(nz,)] * 4 + [(nz, 2)] * 4 + [(y1,)] * 2
     counts += [(nz,)] * 6 + [(3, items)] * 2 + [(4, items)] * 2 + [(nh,)] * 2

time: 78.6 us -> 80.1 us (1.019)
  Pallas kernels: 76 us -> 77 us
    pallas_call x1, Pallas kernels: 76 us -> 77 us  [local(): pl.pallas_call(functools.partial(kernel, nz, ny, nx), out_shape=jax.Shape...]
where the time goes in v3:
time: 80.1 us; the launch traced here: 78.9 us
  Pallas kernels  77 us (96%)
  local copies, waits for them, and re-layouts  1.87 us (2%)
    pallas_call x1, Pallas kernels, local(): pl.pallas_call(functools.partial(kernel, nz, ny, nx), out_shape=jax.Shape...  77 us
    unnamed x1, local copies, waits for them, and re-layouts  1.87 us

profile of v3, /device:TPU:1, one launch (start us, length us, event | category | flops | bytes accessed | tf_op | source)
XLA Modules:
  0.0 78.9 jit_solution(13206961534718737869)
XLA Ops:
  0.0 77.0 %mlstm_layer.1 = bf16[512,512]{1,0:T(8,128)(2,1)} custom-call(bf16[512,256]{1,0:T(8,128)(2,1)} %q_hbm.1, bf16[512,256]{1,0:T(8,128)(2,1)} %k_hbm.1, bf16[512,512]{1,0:T(8,128)(2,1)} %v_hbm.1, f32[1,512]{1,0:T(1,128)} %bitcast.3, f32[1,512]{1,0:T(1,128)} %bitcast.4, f32[1,512]{1,0:T(1,128)} %bitcast.5, bf16[64,512]{1,0:T(8,128)(2,1)} %w_hbm.1), custom_call_target="tpu_custom_call" | custom-call | tf_op jit(solution)/shard_map/mlstm_layer/pallas_call | solution.py:487
  77.0 1.9 %copy.9 = bf16[512,512]{1,0:T(8,128)(2,1)} copy(bf16[512,512]{1,0:T(8,128)(2,1)} %mlstm_layer.1) | data formatting | bytes 1048576

commit v4 on v3

--- a/solution.py
+++ b/solution.py
@@ -11,6 +11,19 @@
 F32 = jnp.float32
 BF16 = jnp.bfloat16
 NY = 4
+
+PLAN = dict(
+    s0=(("ac", 0),),
+    s1=(("wb", 0), ("wa", 1)),
+    s3=(("wb", 1), ("wa", 2), ("ac", -1, 1), ("xr", 0, 1), ("wb", 2), ("wa", 3)),
+    s5a=(("wb", 3), ("wa", 4), ("ac", -2, 2, -3, 3)),
+    s5b=(("xr", 2),),
+    s6=(("wb", 4), ("wa", 5), ("ac", -4, 4), ("rl", 0, -1, 1)),
+    rest=(("wb", 5), ("wa", 6), ("gh", 0), ("xr", 3, 4, 5), ("ac", -5, 5), ("rl", -2, 2), ("wb", 6), ("wa", 7),
+          ("xr", 6), ("rl", -3, 3), ("ac", -6, 6), ("xl", 0, 1, 2), ("wb", 7), ("wa", 8), ("xr", 7),
+          ("xl", 3, 4, 5), ("ac", -7, 7, -8), ("rl", -4, 4), ("xr", 9), ("rl", -5, 5), ("wb", 8), ("xr", 8),
+          ("gh", 1), ("rl", -6, 6), ("gh", 2), ("xl", 6, 7, 9, 8), ("gh", 3), ("rl", -7, 7, -8)),
+)
 
 
 def _log_sigmoid(f):
@@ -104,7 +117,7 @@
 
     partners = [dev(z, yat(d), h) for d in range(1, ny)]
     partners += [dev(zat(d), y, h) for d in range(1, nz)]
-    partners += [(c, lax.rem(h + d, nh)) for d in range(1, nh)]
+    partners += [(c, hat(d)) for d in range(1, nx)] + [(c, sib)]
     barrier = pltpu.get_barrier_semaphore()
     for p in partners:
         pl.semaphore_signal(barrier, inc=1, device_id=p, device_id_type=MESH)
@@ -179,16 +192,11 @@
     def onward(n):
         return 1 if n in (0, 2, 3, 6, 7) else -1
 
-    def x_side(n, slot, hh):
-        piece = item(n, hh)
-        send(piece, piece, bs(slot, n), br(slot, n), (c, sib))
-
     def x_send(n):
         piece = item(n, h)
         if nx > 1:
             send(piece, piece, xs(0, n), xr(0, n), (c, hat(1)))
             send(piece, piece, xs(1, n), xr(1, n), (c, hat(-1)))
-        x_side(n, 0, h)
 
     def x_relay(n):
         if nx > 1:
@@ -197,12 +205,43 @@
                 if onward(n) == -d:
                     piece = item(n, hat(d))
                     send(piece, piece, xs(2, n), xr(2, n), (c, hat(-d)))
-                x_side(n, 1 + slot, hat(d))
 
     def x_last(n):
         if nx > 1:
             take(xr(2, n))
-            x_side(n, 3, hat(2))
+
+    done = set()
+
+    def gate_columns():
+        for d in range(1, nx):
+            take(cr(d - 1))
+        factors = [cbuf[hat(d)] for d in rounds] + [jnp.zeros((128 - 8 * nx, tok), F32)]
+        cols[...] = jnp.transpose(jnp.concatenate(factors, axis=0))
+
+    rounds = (0, -1, 1, 2) if nx > 1 else (0,)
+
+    def gate_head(n):
+        if n < nx:
+            hh = hat(rounds[n])
+            for r in range(2):
+                sl = pl.ds(r * (tok // 2), tok // 2)
+                far_part = jnp.dot(qbuf[hh, sl, :], mbuf[hh], preferred_element_type=F32)
+                near = nbuf[hh, sl, :].astype(F32)
+                gbuf[hh, sl, :] = (
+                    cols[sl, 8 * n:8 * n + 1] * near + cols[sl, 8 * n + 1:8 * n + 2] * far_part
+                ).astype(BF16)
+                piece = gbuf.at[hh, sl, :]
+                send(piece, piece, bs(n, r), br(n, r), (c, sib))
+
+    ops = dict(wa=wa_step, wb=lambda n: wb_step(n) if n else wb_row(), ac=wa_across, rl=wa_relay,
+               xr=x_relay, xl=x_last, gh=gate_head)
+
+    def run(name):
+        for op, *numbers in PLAN[name]:
+            for n in numbers:
+                if (op, n) not in done and (op not in ("xr", "xl") or n < 6 + ny):
+                    done.add((op, n))
+                    ops[op](n)
 
     for load in loads[0:3]:
         load.wait()
@@ -236,7 +275,7 @@
     wb_first()
     x_send(0)
     x_send(1)
-    wa_across(0)
+    run("s0")
 
     loads[5].wait()
     loads[6].wait()
@@ -257,8 +296,7 @@
         to = dev(z, yat(d), h)
         send(sy.at[y], sy.at[y], s1bs(d - 1), s1br(d - 1), to)
         send(mloc.at[yat(d)], ybuf.at[y], s1s(d - 1), s1r(d - 1), to)
-    wb_row()
-    wa_step(1)
+    run("s1")
 
     rb = tok // 4
     dens = []
@@ -275,7 +313,6 @@
         dens.append(jnp.sum(weighted, axis=1, keepdims=True))
         nbuf[h, sl, :] = jnp.dot(
             weighted.astype(BF16), v_ref[0:width, :], preferred_element_type=F32).astype(BF16)
-        x_send(2 + r)
     den_loc = jnp.concatenate(dens, axis=0)
 
     for d in range(1, ny):
@@ -306,16 +343,9 @@
         send(stt, sta.at[z], s3bs(d - 1), s3br(d - 1), to)
         send(tt.at[zat(d)], ta.at[z], s3s(d - 1), s3r(d - 1), to)
 
-    wb_step(1)
-    wa_step(2)
-    wa_across(-1, 1, -2, 2)
-    x_relay(0)
-    x_relay(1)
-    wb_step(2)
-    wa_step(3)
-    wa_relay(0)
-    wb_step(3)
-    wa_step(4)
+    for n in range(2, 6):
+        x_send(n)
+    run("s3")
 
     for d in far:
         take(s3br(d - 1))
@@ -335,10 +365,7 @@
     for d in far:
         send(pb.at[zat(d)], pz.at[z], s5s(d - 1), s5r(d - 1), dev(zat(d), y, h))
 
-    wa_across(-3, 3)
-    x_relay(2)
-    wb_step(4)
-    wa_step(5)
+    run("s5a")
 
     norm_p = sp[z, 0:2, :]
     top_p = sp[z, 2:3, :]
@@ -365,14 +392,10 @@
     which = lax.broadcasted_iota(jnp.int32, (tok, 128), 1)
     both = jnp.where(which == 0, gate * inner, gate * (lift * scale))
     cbuf[h] = jnp.transpose(both)[0:8, :]
-    for d in range(1, nh):
-        send(cbuf.at[h], cbuf.at[h], cs(d - 1), cr(d - 1), (c, lax.rem(h + d, nh)))
-
-    x_relay(3)
-    wb_step(5)
-    wa_step(6)
-    wa_across(-4, 4)
-    wa_relay(-1, 1)
+    for d in range(1, nx):
+        send(cbuf.at[h], cbuf.at[h], cs(d - 1), cr(d - 1), (c, hat(d)))
+
+    run("s5b")
 
     for d in far:
         take(s5r(d - 1))
@@ -389,56 +412,17 @@
         send(mo.at[yat(d)], mbuf.at[h, own_quarter, :], s6s(d - 1), s6r(d - 1), dev(z, yat(d), h))
     x_send(6)
 
-    wb_step(6)
-    wa_step(7)
-    x_relay(4)
-    x_relay(5)
+    run("s6")
 
     for d in sorted(range(1, ny), key=lambda d: min(d, ny - d)):
         take(s6r(d - 1))
         x_send(6 + d)
-    for n in range(2, 6):
-        x_last(n)
-    x_last(0)
-    x_last(1)
-    wa_across(-5, 5, -6, 6)
-    wa_relay(-2, 2)
-    wb_step(7)
-    wa_step(8)
-    wb_step(8)
-    wa_across(-7, 7, -8)
-    wa_relay(-3, 3)
-    order = [6] + [6 + d for d in sorted(range(1, ny), key=lambda d: min(d, ny - d))]
-    for n, js in zip(order, ((-4, 4), (-5, 5), (-6, 6), (-7,))):
-        x_relay(n)
-        wa_relay(*js)
-    wa_relay(*((7, -8) if ny > 1 else ()))
-    for n in order:
-        x_last(n)
-
-    for d in range(1, nh):
-        take(cr(d - 1))
-    heads = [(0, h, None), (1, sib, 0)]
-    if nx > 1:
-        heads += [(2, hat(-1), None), (3, hat(-1, 1), 1), (4, hat(1), None), (5, hat(1, 1), 2),
-                  (6, hat(2), None), (7, hat(2, 1), 3)]
-    factors = [cbuf[hh] for _, hh, _ in heads]
-    if nh < 16:
-        factors += [jnp.zeros((128 - 8 * nh, tok), F32)]
-    cols[...] = jnp.transpose(jnp.concatenate(factors, axis=0))
-    items = range(6 + ny)
-    for n, hh, slot in heads:
-        if slot is not None:
-            for m in items:
-                take(br(slot, m))
+    gate_columns()
+    run("rest")
+
+    for n in range(nx):
         for r in range(2):
-            sl = pl.ds(r * (tok // 2), tok // 2)
-            far_part = jnp.dot(qbuf[hh, sl, :], mbuf[hh], preferred_element_type=F32)
-            near = nbuf[hh, sl, :].astype(F32)
-            gbuf[hh, sl, :] = (
-                cols[sl, 8 * n:8 * n + 1] * near + cols[sl, 8 * n + 1:8 * n + 2] * far_part
-            ).astype(BF16)
-
+            take(br(n, r))
     if ny > 1:
         for j in rels:
             take(y2r(j + nf))
@@ -482,7 +466,7 @@
         v((nh, tok, dv), BF16), v((nh * dv // w_out.shape[0],) + w_out.shape, BF16),
     ]
     counts = [(y1,)] * 4 + [(z1,)] * 6 + [(y1,)] * 2 + [(nz,)] * 4 + [(nz, 2)] * 4 + [(y1,)] * 2
-    counts += [(nz,)] * 6 + [(3, items)] * 2 + [(4, items)] * 2 + [(nh,)] * 2
+    counts += [(nz,)] * 6 + [(3, items)] * 2 + [(nx, 2)] * 2 + [(nh,)] * 2
     scratch += [pltpu.SemaphoreType.DMA(n) for n in counts]
     return pl.pallas_call(
         functools.partial(kernel, nz, ny, nx),

time: 80.1 us -> 75.5 us (0.943)
  Pallas kernels: 77 us -> 72.3 us
    pallas_call x1, Pallas kernels: 77 us -> 72.3 us  [local(): pl.pallas_call(functools.partial(kernel, nz, ny, nx), out_shape=jax.Shape...]
where the time goes in v4:
time: 75.5 us; the launch traced here: 74.2 us
  Pallas kernels  72.3 us (96%)
  local copies, waits for them, and re-layouts  1.87 us (2%)
    pallas_call x1, Pallas kernels, local(): pl.pallas_call(functools.partial(kernel, nz, ny, nx), out_shape=jax.Shape...  72.3 us
    unnamed x1, local copies, waits for them, and re-layouts  1.87 us

profile of v4, /device:TPU:1, one launch (start us, length us, event | category | flops | bytes accessed | tf_op | source)
XLA Modules:
  0.0 74.2 jit_solution(5413107420484763735)
XLA Ops:
  0.0 72.3 %mlstm_layer.1 = bf16[512,512]{1,0:T(8,128)(2,1)} custom-call(bf16[512,256]{1,0:T(8,128)(2,1)} %q_hbm.1, bf16[512,256]{1,0:T(8,128)(2,1)} %k_hbm.1, bf16[512,512]{1,0:T(8,128)(2,1)} %v_hbm.1, f32[1,512]{1,0:T(1,128)} %bitcast.3, f32[1,512]{1,0:T(1,128)} %bitcast.4, f32[1,512]{1,0:T(1,128)} %bitcast.5, bf16[64,512]{1,0:T(8,128)(2,1)} %w_hbm.1), custom_call_target="tpu_custom_call" | custom-call | tf_op jit(solution)/shard_map/mlstm_layer/pallas_call | solution.py:471
  72.4 1.9 %copy.9 = bf16[512,512]{1,0:T(8,128)(2,1)} copy(bf16[512,512]{1,0:T(8,128)(2,1)} %mlstm_layer.1) | data formatting | bytes 1048576

commit v5 on v4

--- a/solution.py
+++ b/solution.py
@@ -13,16 +13,15 @@
 NY = 4
 
 PLAN = dict(
-    s0=(("ac", 0),),
-    s1=(("wb", 0), ("wa", 1)),
-    s3=(("wb", 1), ("wa", 2), ("ac", -1, 1), ("xr", 0, 1), ("wb", 2), ("wa", 3)),
-    s5a=(("wb", 3), ("wa", 4), ("ac", -2, 2, -3, 3)),
-    s5b=(("xr", 2),),
-    s6=(("wb", 4), ("wa", 5), ("ac", -4, 4), ("rl", 0, -1, 1)),
-    rest=(("wb", 5), ("wa", 6), ("gh", 0), ("xr", 3, 4, 5), ("ac", -5, 5), ("rl", -2, 2), ("wb", 6), ("wa", 7),
-          ("xr", 6), ("rl", -3, 3), ("ac", -6, 6), ("xl", 0, 1, 2), ("wb", 7), ("wa", 8), ("xr", 7),
-          ("xl", 3, 4, 5), ("ac", -7, 7, -8), ("rl", -4, 4), ("xr", 9), ("rl", -5, 5), ("wb", 8), ("xr", 8),
-          ("gh", 1), ("rl", -6, 6), ("gh", 2), ("xl", 6, 7, 9, 8), ("gh", 3), ("rl", -7, 7, -8)),
+    gates=(("wb", 0), ("wa", 1)),
+    s1=(("wb", 1), ("wa", 2)),
+    s3=(("ac", -1, 1), ("wb", 2), ("wa", 3), ("xr", 0, 1), ("ac", -2, 2), ("rl", 0), ("wb", 3), ("wa", 4)),
+    s5a=(("ac", -3, 3), ("wb", 4), ("wa", 5)),
+    s5b=(("ac", -4, 4), ("rl", -1, 1), ("xr", 2), ("wb", 5), ("wa", 6)),
+    s6=(("ac", -5, 5), ("rl", -2, 2), ("wb", 6), ("wa", 7), ("ac", -6, 6)),
+    rest=(("xr", 3), ("rl", -3, 3), ("gh", 0), ("xr", 4, 5), ("wb", 7), ("wa", 8), ("ac", -7, 7, -8), ("xr", 6),
+          ("rl", -4, 4), ("xl", 0, 1), ("xr", 7, 9), ("rl", -5, 5), ("xl", 2, 3, 4, 5), ("wb", 8), ("xr", 8),
+          ("gh", 1), ("rl", -6, 6), ("gh", 2), ("rl", -7, 7, -8), ("xl", 6, 7, 9, 8), ("gh", 3)),
 )
 
 
@@ -97,8 +96,8 @@
 
     loads = [
         pltpu.make_async_copy(src, dst, ins.at[n]) for n, (src, dst) in enumerate((
-            (f_hbm, f_ref), (i_hbm, i_ref), (o_hbm, o_ref), (w_hbm, wbuf.at[c]),
-            (q_hbm, qbuf.at[h]), (k_hbm, k_ref), (v_hbm, v_ref)))
+            (w_hbm, wbuf.at[c]), (f_hbm, f_ref), (i_hbm, i_ref), (o_hbm, o_ref),
+            (k_hbm, k_ref), (v_hbm, v_ref), (q_hbm, qbuf.at[h])))
     ]
     for load in loads:
         load.start()
@@ -243,7 +242,13 @@
                     done.add((op, n))
                     ops[op](n)
 
-    for load in loads[0:3]:
+    loads[0].wait()
+    pl.semaphore_wait(barrier, len(partners))
+    wa_step(0)
+    wb_first()
+    wa_across(0)
+
+    for load in loads[1:4]:
         load.wait()
     lane = lax.broadcasted_iota(jnp.int32, (8, tok), 1)
     gate_in = jnp.broadcast_to(i_ref[...], (8, tok))
@@ -267,18 +272,10 @@
             jnp.where(rows == 2, sig[0:1], kw_row[0:1])))
     cols[...] = jnp.transpose(stack)
     a1 = a_row[0:1]
-    loads[3].wait()
+    run("gates")
+
     loads[4].wait()
-
-    pl.semaphore_wait(barrier, len(partners))
-    wa_step(0)
-    wb_first()
-    x_send(0)
-    x_send(1)
-    run("s0")
-
     loads[5].wait()
-    loads[6].wait()
     scaled = k_ref[...].astype(F32) * cols[:, 3:4]
     norm = jnp.sum(scaled, axis=0, keepdims=True)
     m_local = lax.dot_general(
@@ -296,6 +293,9 @@
         to = dev(z, yat(d), h)
         send(sy.at[y], sy.at[y], s1bs(d - 1), s1br(d - 1), to)
         send(mloc.at[yat(d)], ybuf.at[y], s1s(d - 1), s1r(d - 1), to)
+    loads[6].wait()
+    x_send(0)
+    x_send(1)
     run("s1")
 
     rb = tok // 4

time: 75.5 us -> 74.2 us (0.983); the launches traced: 74.2 us -> 74 us
  no operation moved by 1% of the time
where the time goes in v5:
time: 74.2 us; the launch traced here: 74 us
  Pallas kernels  72.2 us (97%)
  local copies, waits for them, and re-layouts  1.87 us (3%)
    pallas_call x1, Pallas kernels, local(): pl.pallas_call(functools.partial(kernel, nz, ny, nx), out_shape=jax.Shape...  72.2 us
    unnamed x1, local copies, waits for them, and re-layouts  1.87 us

profile of v5, /device:TPU:1, one launch (start us, length us, event | category | flops | bytes accessed | tf_op | source)
XLA Modules:
  0.0 74.0 jit_solution(10747917301580625153)
XLA Ops:
  0.0 72.2 %mlstm_layer.1 = bf16[512,512]{1,0:T(8,128)(2,1)} custom-call(bf16[512,256]{1,0:T(8,128)(2,1)} %q_hbm.1, bf16[512,256]{1,0:T(8,128)(2,1)} %k_hbm.1, bf16[512,512]{1,0:T(8,128)(2,1)} %v_hbm.1, f32[1,512]{1,0:T(1,128)} %bitcast.3, f32[1,512]{1,0:T(1,128)} %bitcast.4, f32[1,512]{1,0:T(1,128)} %bitcast.5, bf16[64,512]{1,0:T(8,128)(2,1)} %w_hbm.1), custom_call_target="tpu_custom_call" | custom-call | tf_op jit(solution)/shard_map/mlstm_layer/pallas_call | solution.py:471
  72.2 1.9 %copy.9 = bf16[512,512]{1,0:T(8,128)(2,1)} copy(bf16[512,512]{1,0:T(8,128)(2,1)} %mlstm_layer.1) | data formatting | bytes 1048576

commit v6 on v5

--- a/solution.py
+++ b/solution.py
@@ -20,8 +20,8 @@
     s5b=(("ac", -4, 4), ("rl", -1, 1), ("xr", 2), ("wb", 5), ("wa", 6)),
     s6=(("ac", -5, 5), ("rl", -2, 2), ("wb", 6), ("wa", 7), ("ac", -6, 6)),
     rest=(("xr", 3), ("rl", -3, 3), ("gh", 0), ("xr", 4, 5), ("wb", 7), ("wa", 8), ("ac", -7, 7, -8), ("xr", 6),
-          ("rl", -4, 4), ("xl", 0, 1), ("xr", 7, 9), ("rl", -5, 5), ("xl", 2, 3, 4, 5), ("wb", 8), ("xr", 8),
-          ("gh", 1), ("rl", -6, 6), ("gh", 2), ("rl", -7, 7, -8), ("xl", 6, 7, 9, 8), ("gh", 3)),
+          ("rl", -4, 4, -5, 5), ("xl", 0, 1, 2, 3, 4, 5), ("xr", 7, 9), ("rl", -6, 6), ("xl", 6), ("rl", -7, 7, -8),
+          ("xr", 8), ("gh", 1, 2), ("xl", 7, 9, 8), ("gh", 3), ("wb", 8)),
 )
 
 
@@ -54,7 +54,7 @@
 
 def kernel(nz, ny, nx, q_hbm, k_hbm, v_hbm, i_hbm, f_hbm, o_hbm, w_hbm, out_ref, *scr):
     (k_ref, v_ref, i_ref, f_ref, o_ref, ins, mloc, ybuf, sy, tt, stt, ta, sta, pb, sp, pz, mo, sm, cols,
-     qbuf, nbuf, mbuf, cbuf, gbuf, wbuf, *sems) = scr
+     qbuf, nbuf, mbuf, cbuf, gbuf, wbuf, acc, *sems) = scr
     (s1s, s1r, s1bs, s1br, s3s, s3r, s3bs, s3br, s5s, s5r, s6s, s6r, wafs, wafr, wabs, wabr,
      wbfs, wbfr, wbbs, wbbr, w0s, w0r, yps, ypr, yms, ymr, y2s, y2r, xs, xr, bs, br, cs, cr) = [
         Sems(n, ref) for n, ref in enumerate(sems)]
@@ -420,24 +420,29 @@
     gate_columns()
     run("rest")
 
+    if ny > 1:
+        for j in rels:
+            take(y2r(j + nf))
+
+    def weights(hh):
+        if wr >= dv:
+            row = pl.multiple_of(lax.rem(hh * dv, wr), dv)
+            return wbuf[lax.div(hh * dv, wr), pl.ds(row, dv), :]
+        return wbuf[pl.ds(hh * (dv // wr), dv // wr)].reshape(dv, dv)
+
+    def project(sl, other):
+        return sum(
+            jnp.dot(gbuf[hat(d, other), sl, :], weights(hat(d, other)), preferred_element_type=F32)
+            for d in rounds)
+
+    row_halves = [pl.ds(r * (tok // 2), tok // 2) for r in range(2)]
+    for sl in row_halves:
+        acc[sl, :] = project(sl, 0)
     for n in range(nx):
         for r in range(2):
             take(br(n, r))
-    if ny > 1:
-        for j in rels:
-            take(y2r(j + nf))
-
-    if wr >= dv:
-        weights = [wbuf[hh * dv // wr, hh * dv % wr:hh * dv % wr + dv, :] for hh in range(nh)]
-    else:
-        per = dv // wr
-        weights = [wbuf[hh * per:(hh + 1) * per].reshape(dv, dv) for hh in range(nh)]
-    for rr in range(tok // 256):
-        sl = slice(rr * 256, (rr + 1) * 256)
-        acc = jnp.zeros((256, dv), F32)
-        for hh in range(nh):
-            acc = acc + jnp.dot(gbuf[hh, sl, :], weights[hh], preferred_element_type=F32)
-        out_ref[sl, :] = acc.astype(BF16)
+    for sl in row_halves:
+        out_ref[sl, :] = (acc[sl, :] + project(sl, 1)).astype(BF16)
 
     assert set(started) == got
     for copy in started.values():
@@ -464,6 +469,7 @@
         v((tok, 128), F32),
         v((nh, tok, dk), BF16), v((nh, tok, dv), BF16), v((nh, dk, dv), BF16), v((nh, 8, tok), F32),
         v((nh, tok, dv), BF16), v((nh * dv // w_out.shape[0],) + w_out.shape, BF16),
+        v((tok, dv), F32),
     ]
     counts = [(y1,)] * 4 + [(z1,)] * 6 + [(y1,)] * 2 + [(nz,)] * 4 + [(nz, 2)] * 4 + [(y1,)] * 2
     counts += [(nz,)] * 6 + [(3, items)] * 2 + [(nx, 2)] * 2 + [(nh,)] * 2

time: 74.2 us -> 74.1 us (level)
  no operation moved by 1% of the time
where the time goes in v6:
time: 74.1 us; the launch traced here: 74 us
  Pallas kernels  72.1 us (97%)
  local copies, waits for them, and re-layouts  1.87 us (3%)
    pallas_call x1, Pallas kernels, local(): pl.pallas_call(functools.partial(kernel, nz, ny, nx), out_shape=jax.Shape...  72.1 us
    unnamed x1, local copies, waits for them, and re-layouts  1.87 us

profile of v6, /device:TPU:1, one launch (start us, length us, event | category | flops | bytes accessed | tf_op | source)
XLA Modules:
  0.0 74.0 jit_solution(9313766364635218011)
XLA Ops:
  0.0 72.1 %mlstm_layer.1 = bf16[512,512]{1,0:T(8,128)(2,1)} custom-call(bf16[512,256]{1,0:T(8,128)(2,1)} %q_hbm.1, bf16[512,256]{1,0:T(8,128)(2,1)} %k_hbm.1, bf16[512,512]{1,0:T(8,128)(2,1)} %v_hbm.1, f32[1,512]{1,0:T(1,128)} %bitcast.3, f32[1,512]{1,0:T(1,128)} %bitcast.4, f32[1,512]{1,0:T(1,128)} %bitcast.5, bf16[64,512]{1,0:T(8,128)(2,1)} %w_hbm.1), custom_call_target="tpu_custom_call" | custom-call | tf_op jit(solution)/shard_map/mlstm_layer/pallas_call | solution.py:477
  72.1 1.9 %copy.9 = bf16[512,512]{1,0:T(8,128)(2,1)} copy(bf16[512,512]{1,0:T(8,128)(2,1)} %mlstm_layer.1) | data formatting | bytes 1048576

commit v7 on v6

--- a/solution.py
+++ b/solution.py
@@ -96,8 +96,8 @@
 
     loads = [
         pltpu.make_async_copy(src, dst, ins.at[n]) for n, (src, dst) in enumerate((
-            (w_hbm, wbuf.at[c]), (f_hbm, f_ref), (i_hbm, i_ref), (o_hbm, o_ref),
-            (k_hbm, k_ref), (v_hbm, v_ref), (q_hbm, qbuf.at[h])))
+            (w_hbm, wbuf.at[c]), (q_hbm, qbuf.at[h]), (f_hbm, f_ref), (i_hbm, i_ref), (o_hbm, o_ref),
+            (k_hbm, k_ref), (v_hbm, v_ref)))
     ]
     for load in loads:
         load.start()
@@ -247,8 +247,11 @@
     wa_step(0)
     wb_first()
     wa_across(0)
-
-    for load in loads[1:4]:
+    loads[1].wait()
+    x_send(0)
+    x_send(1)
+
+    for load in loads[2:5]:
         load.wait()
     lane = lax.broadcasted_iota(jnp.int32, (8, tok), 1)
     gate_in = jnp.broadcast_to(i_ref[...], (8, tok))
@@ -274,8 +277,8 @@
     a1 = a_row[0:1]
     run("gates")
 
-    loads[4].wait()
     loads[5].wait()
+    loads[6].wait()
     scaled = k_ref[...].astype(F32) * cols[:, 3:4]
     norm = jnp.sum(scaled, axis=0, keepdims=True)
     m_local = lax.dot_general(
@@ -293,9 +296,6 @@
         to = dev(z, yat(d), h)
         send(sy.at[y], sy.at[y], s1bs(d - 1), s1br(d - 1), to)
         send(mloc.at[yat(d)], ybuf.at[y], s1s(d - 1), s1r(d - 1), to)
-    loads[6].wait()
-    x_send(0)
-    x_send(1)
     run("s1")
 
     rb = tok // 4
@@ -343,8 +343,8 @@
         send(stt, sta.at[z], s3bs(d - 1), s3br(d - 1), to)
         send(tt.at[zat(d)], ta.at[z], s3s(d - 1), s3r(d - 1), to)
 
-    for n in range(2, 6):
-        x_send(n)
+    x_send(2)
+    x_send(3)
     run("s3")
 
     for d in far:
@@ -365,6 +365,8 @@
     for d in far:
         send(pb.at[zat(d)], pz.at[z], s5s(d - 1), s5r(d - 1), dev(zat(d), y, h))
 
+    x_send(4)
+    x_send(5)
     run("s5a")
 
     norm_p = sp[z, 0:2, :]

time: 74.1 us -> 74.7 us (level)
  no operation moved by 1% of the time
where the time goes in v7:
time: 74.7 us; the launch traced here: 74.5 us
  Pallas kernels  72.6 us (97%)
  local copies, waits for them, and re-layouts  1.87 us (3%)
    pallas_call x1, Pallas kernels, local(): pl.pallas_call(functools.partial(kernel, nz, ny, nx), out_shape=jax.Shape...  72.6 us
    unnamed x1, local copies, waits for them, and re-layouts  1.87 us

profile of v7, /device:TPU:1, one launch (start us, length us, event | category | flops | bytes accessed | tf_op | source)
XLA Modules:
  0.0 74.5 jit_solution(522225919641468701)
XLA Ops:
  0.0 72.6 %mlstm_layer.1 = bf16[512,512]{1,0:T(8,128)(2,1)} custom-call(bf16[512,256]{1,0:T(8,128)(2,1)} %q_hbm.1, bf16[512,256]{1,0:T(8,128)(2,1)} %k_hbm.1, bf16[512,512]{1,0:T(8,128)(2,1)} %v_hbm.1, f32[1,512]{1,0:T(1,128)} %bitcast.3, f32[1,512]{1,0:T(1,128)} %bitcast.4, f32[1,512]{1,0:T(1,128)} %bitcast.5, bf16[64,512]{1,0:T(8,128)(2,1)} %w_hbm.1), custom_call_target="tpu_custom_call" | custom-call | tf_op jit(solution)/shard_map/mlstm_layer/pallas_call | solution.py:479
  72.6 1.9 %copy.9 = bf16[512,512]{1,0:T(8,128)(2,1)} copy(bf16[512,512]{1,0:T(8,128)(2,1)} %mlstm_layer.1) | data formatting | bytes 1048576
